TPU v7x, 32 devices: a whole 2x2x4 slice. The times are simulated.
32 devices in a mesh: groups: 2 (over y), seq: 8 (over z, x), enc: 2 (over core).
Axes of the slice: x: 2, y: 2, z: 4, core: 2. Of those that a mesh axis runs over, the one named last changes fastest.
Arguments:
- self_queries: bfloat16 [2, 256, 4096], P('enc', ('groups', 'seq')), parts along dimension 1, may hold values from -32 to 32
- self_keys: bfloat16 [2, 256, 4096], P('enc', ('groups', 'seq')), parts along dimension 1, may hold values from -32 to 32
- self_values: bfloat16 [2, 256, 4096], P('enc', ('groups', 'seq')), parts along dimension 1, may hold values from -6 to 6
- text_queries: bfloat16 [2, 256, 4096], P('enc', ('groups', 'seq')), parts along dimension 1, may hold values from -32 to 32
- text_kv: bfloat16 [2, 2, 1024, 4096], P('enc', None, ('groups', 'seq')), parts along dimension 2, may hold values from -32 to 32
- text_len: int32 [4], P('groups'), parts along dimension 0, may hold values from 16 to 512
Outputs:
- self_mixed: bfloat16 [2, 256, 4096], P('enc', ('groups', 'seq')), parts along dimension 1
- text_mixed: bfloat16 [2, 256, 4096], P('enc', ('groups', 'seq')), parts along dimension 1
There are 2 independent parts, one for each index of `groups`. A program takes and returns all parts, laid end to end along the dimension named above; each array names one. Nothing has to cross between parts.
Inputs may be any that keep to these rules, and one draw needn't show every extreme that they name: `text_len`: entry 0 is the prompt's length, entry 1 the negative prompt's; text rows at or past a length are padding.
All inputs are finite; a program needn't handle non-finite values.
Results may differ from a plain program's by a relative error of at most 0.0034.
Values may be sent and summed in bfloat16 or wider, within the bound.
A program may use at most 64 MiB of HBM per device.

v0:
```python
import functools
import math

import jax
import jax.numpy as jnp
from jax import lax
from jax.experimental import pallas as pl
from jax.experimental.pallas import tpu as pltpu
from jax.sharding import PartitionSpec as P

HEADS = 32
HEAD_DIM = 128


def absorb(run_state, queries, key_rows, value_rows, live_mask):
    running_max, row_total, weighted_sum = run_state
    scores = jnp.einsum(
        "qpd,kpd->pqk", queries, key_rows, preferred_element_type=jnp.float32
    ) / math.sqrt(HEAD_DIM)
    scores = jnp.where(live_mask[None, None, :], scores, -1e30)
    new_max = jnp.maximum(running_max, jnp.max(scores, axis=2))
    weights = jnp.where(live_mask[None, None, :], jnp.exp(scores - new_max[:, :, None]), 0.0)
    factor = jnp.exp(running_max - new_max)
    row_total = row_total * factor + jnp.sum(weights, axis=2)
    weighted_sum = weighted_sum * factor[:, :, None] + jnp.einsum(
        "pqk,kpd->pqd", weights.astype(jnp.bfloat16), value_rows, preferred_element_type=jnp.float32
    )
    return (new_max, row_total, weighted_sum)


def empty_state(head_count, query_count):
    return (
        jnp.full((head_count, query_count), -1e30, jnp.float32),
        jnp.zeros((head_count, query_count), jnp.float32),
        jnp.zeros((head_count, query_count, HEAD_DIM), jnp.float32),
    )


def finish(run_state):
    running_max, row_total, weighted_sum = run_state
    return (weighted_sum / row_total[:, :, None]).transpose(1, 0, 2).astype(jnp.bfloat16)


def block_attention(queries, key_rows, value_rows, live_mask):
    query_total, heads_here, head_width = queries.shape
    key_total = key_rows.shape[0]
    key_block = 1024 if key_total % 1024 == 0 else key_total
    query_block = 512 if query_total % 512 == 0 else query_total
    key_blocks = key_rows.reshape(key_total // key_block, key_block, heads_here, head_width)
    value_blocks = value_rows.reshape(key_total // key_block, key_block, heads_here, head_width)
    live_blocks = live_mask.reshape(key_total // key_block, key_block)

    def one_block(query_piece):

        def absorb_block(run_state, pieces):
            return (absorb(run_state, query_piece, pieces[0], pieces[1], pieces[2]), None)

        final_state, unused = lax.scan(
            absorb_block,
            empty_state(heads_here, query_block),
            (key_blocks, value_blocks, live_blocks),
        )
        return finish(final_state)

    blended = lax.map(
        one_block, queries.reshape(query_total // query_block, query_block, heads_here, head_width)
    )
    return blended.reshape(query_total, heads_here, head_width)


def shards(self_queries, self_keys, self_values, text_queries, text_kv, text_len):
    token_rows = self_queries.shape[1]
    channel_count = self_queries.shape[2]
    seq_count = lax.axis_size("seq")
    quarter_count = max(seq_count // HEADS, 1)
    heads_here = max(HEADS // seq_count, 1)
    group_count = HEADS // heads_here
    head_span = heads_here * HEAD_DIM
    share_rows = token_rows // quarter_count
    query_total = share_rows * seq_count
    branch = lax.axis_index("enc")
    length = lax.dynamic_index_in_dim(text_len, branch, 0, keepdims=False)

    def head_view(tensor):
        return tensor.reshape(1, share_rows, seq_count, head_span)

    def repeated(tensor):
        spread = jnp.broadcast_to(
            tensor.reshape(1, token_rows, 1, group_count, head_span),
            (1, token_rows, quarter_count, group_count, head_span),
        )
        return spread.reshape(1, token_rows, seq_count, head_span)

    head_queries, head_keys, head_values = (
        lax.all_to_all(head_view(self_queries), "seq", split_axis=2, concat_axis=1, tiled=True),
        lax.all_to_all(repeated(self_keys), "seq", split_axis=2, concat_axis=1, tiled=True),
        lax.all_to_all(repeated(self_values), "seq", split_axis=2, concat_axis=1, tiled=True),
    )
    key_rows = head_keys.reshape(-1, heads_here, HEAD_DIM)
    value_rows = head_values.reshape(-1, heads_here, HEAD_DIM)
    query_rows = head_queries.reshape(query_total, heads_here, HEAD_DIM)
    every_key = jnp.ones((key_rows.shape[0],), jnp.bool_)
    self_heads = block_attention(query_rows, key_rows, value_rows, every_key)
    head_text_queries = lax.all_to_all(
        head_view(text_queries), "seq", split_axis=2, concat_axis=1, tiled=True
    )
    context_rows = text_kv.shape[2]
    spread = jnp.broadcast_to(
        text_kv.reshape(1, 2, context_rows, 1, group_count, head_span),
        (1, 2, context_rows, quarter_count, group_count, head_span),
    )
    head_context = lax.all_to_all(
        spread.reshape(1, 2, context_rows, seq_count, head_span),
        "seq",
        split_axis=3,
        concat_axis=2,
        tiled=True,
    )
    text_total = head_context.shape[2]
    context_keys = head_context[0, 0].reshape(text_total, heads_here, HEAD_DIM)
    context_values = head_context[0, 1].reshape(text_total, heads_here, HEAD_DIM)
    live_mask = jnp.arange(text_total, dtype=jnp.int32) < length
    text_heads = block_attention(
        head_text_queries.reshape(query_total, heads_here, HEAD_DIM),
        context_keys,
        context_values,
        live_mask,
    )
    self_view = self_heads.reshape(1, seq_count, share_rows, 1, head_span)
    text_view = text_heads.reshape(1, seq_count, share_rows, 1, head_span)
    self_back, text_back = (
        lax.all_to_all(self_view, "seq", split_axis=1, concat_axis=3, tiled=True),
        lax.all_to_all(text_view, "seq", split_axis=1, concat_axis=3, tiled=True),
    )
    self_mixed = self_back.reshape(1, token_rows, channel_count)
    text_mixed = text_back.reshape(1, token_rows, channel_count)
    return (self_mixed, text_mixed)


HALVES = 2
MESH = pl.DeviceIdType.MESH
FAR = -1e30


def attend(queries, key_rows, value_rows, live):
    scores = lax.dot_general(
        queries, key_rows, (((1,), (1,)), ((), ())), preferred_element_type=jnp.float32
    ) * (1.0 / math.sqrt(HEAD_DIM))
    if live is not None:
        scores = jnp.where(live, scores, FAR)
    top = jnp.max(scores, axis=1, keepdims=True)
    weights = jnp.exp(scores - top)
    if live is not None:
        weights = jnp.where(live, weights, 0.0)
    total = jnp.sum(weights, axis=1, keepdims=True)
    mixed = jnp.dot(weights.astype(jnp.bfloat16), value_rows, preferred_element_type=jnp.float32)
    return mixed, top, total


def fused(
    count,
    self_q,
    self_k,
    self_v,
    text_q,
    text_kv,
    text_len,
    self_out,
    text_out,
    own_q,
    own_k,
    own_v,
    text_rows,
    context,
    self_part,
    text_part,
    stat_part,
    text_back,
    stat_back,
    stat_cols,
    send_sem,
    recv_sem,
    local_sem,
):
    me = lax.axis_index("seq")
    branch = lax.axis_index("enc")
    ring = count // HALVES
    half, place = lax.div(me, ring), lax.rem(me, ring)
    rows = self_q.shape[1]
    query_total = count * rows
    context_rows = text_kv.shape[2]
    key_total = ring * context_rows
    self_span = own_q.shape[2]
    text_span = text_rows.shape[2]
    self_heads, text_heads = self_span // HEAD_DIM, text_span // HEAD_DIM

    def peer(step):
        return lax.rem(me + step, count)

    def near(step):
        return half * ring + lax.rem(place + step, ring)

    def self_cols(device):
        return pl.ds(pl.multiple_of(device * self_span, self_span), self_span)

    def text_cols(device):
        return pl.ds(pl.multiple_of(lax.rem(device, ring) * text_span, text_span), text_span)

    def remote(kind, step, source, target, device):
        return pltpu.make_async_remote_copy(
            src_ref=source,
            dst_ref=target,
            send_sem=send_sem.at[kind, step],
            recv_sem=recv_sem.at[kind, step],
            device_id={"seq": device},
            device_id_type=MESH,
        )

    kept = [
        pltpu.make_async_copy(text_q.at[0, :, text_cols(me)], text_rows.at[me], local_sem.at[0]),
        pltpu.make_async_copy(text_kv.at[0, :, :, text_cols(me)], context.at[place], local_sem.at[1]),
        pltpu.make_async_copy(self_q.at[0, :, self_cols(me)], own_q.at[me], local_sem.at[2]),
        pltpu.make_async_copy(self_k.at[0, :, self_cols(me)], own_k.at[me], local_sem.at[3]),
        pltpu.make_async_copy(self_v.at[0, :, self_cols(me)], own_v.at[me], local_sem.at[4]),
    ]
    for copy in kept:
        copy.start()

    barrier = pltpu.get_barrier_semaphore()
    for step in range(1, count):
        pl.semaphore_signal(barrier, inc=1, device_id={"seq": peer(step)}, device_id_type=MESH)
    pl.semaphore_wait(barrier, count - 1)

    text_in, self_in = [], []
    for step in range(1, count):
        to = peer(step)
        text_in.append(remote(0, step, text_q.at[0, :, text_cols(to)], text_rows.at[me], to))
    for step in range(1, ring):
        to = near(step)
        text_in.append(remote(1, step, text_kv.at[0, :, :, text_cols(to)], context.at[place], to))
    for kind, source, target in ((2, self_q, own_q), (3, self_k, own_k), (4, self_v, own_v)):
        for step in range(1, count):
            to = peer(step)
            self_in.append(remote(kind, step, source.at[0, :, self_cols(to)], target.at[me], to))
    order = [kind * (count - 1) + step - 1 for step in range(1, count) for kind in range(3)]
    for copy in text_in + [self_in[n] for n in order]:
        copy.start()

    for copy in kept[:2]:
        copy.wait()
    for copy in text_in:
        copy.wait_recv()
    length = text_len[branch]
    live = half * key_total + lax.broadcasted_iota(jnp.int32, (1, key_total), 1) < length
    lane = lax.broadcasted_iota(jnp.int32, (query_total, HEAD_DIM), 1)
    stats = jnp.full((query_total, HEAD_DIM), FAR, jnp.float32)
    for head in range(text_heads):
        span = slice(head * HEAD_DIM, (head + 1) * HEAD_DIM)
        mixed, top, total = attend(
            text_rows[:, :, span].reshape(query_total, HEAD_DIM),
            context[:, 0, :, span].reshape(key_total, HEAD_DIM),
            context[:, 1, :, span].reshape(key_total, HEAD_DIM),
            live,
        )
        safe = jnp.where(total > 0.0, total, 1.0)
        weight = jnp.where(total > 0.0, top + jnp.log(safe), FAR)
        text_part[:, :, span] = (mixed / safe).astype(jnp.bfloat16).reshape(count, rows, HEAD_DIM)
        stats = jnp.where(lane == head, weight, stats)
    stat_part[...] = stats.T[:text_heads]
    kept.append(pltpu.make_async_copy(text_part.at[me], text_back.at[half, :, text_cols(me)], local_sem.at[5]))
    kept.append(pltpu.make_async_copy(stat_part, stat_back.at[me], local_sem.at[6]))
    kept[5].start()
    kept[6].start()
    text_return = []
    for step in range(1, count):
        to = peer(step)
        text_return.append(remote(6, step, stat_part, stat_back.at[me], to))
        text_return.append(remote(5, step, text_part.at[to], text_back.at[half, :, text_cols(me)], to))
    for copy in text_return:
        copy.start()

    for copy in kept[2:5]:
        copy.wait()
    for copy in self_in:
        copy.wait_recv()
    for head in range(self_heads):
        span = slice(head * HEAD_DIM, (head + 1) * HEAD_DIM)
        mixed, top, total = attend(
            own_q[:, :, span].reshape(query_total, HEAD_DIM),
            own_k[:, :, span].reshape(query_total, HEAD_DIM),
            own_v[:, :, span].reshape(query_total, HEAD_DIM),
            None,
        )
        self_part[:, :, span] = (mixed / total).astype(jnp.bfloat16).reshape(count, rows, HEAD_DIM)
    kept.append(pltpu.make_async_copy(self_part.at[me], self_out.at[0, :, self_cols(me)], local_sem.at[7]))
    kept[7].start()
    self_return = []
    for step in range(1, count):
        to = peer(step)
        self_return.append(remote(7, step, self_part.at[to], self_out.at[0, :, self_cols(me)], to))
    for copy in self_return:
        copy.start()

    kept[5].wait()
    kept[6].wait()
    for copy in text_return:
        copy.wait_recv()
    stat_cols[...] = stat_back[...].reshape(HALVES * HEADS, query_total).T
    mine = stat_cols[pl.ds(pl.multiple_of(me * rows, rows), rows), :]
    sides = [mine[:, side * HEADS : (side + 1) * HEADS] for side in range(HALVES)]
    highest = functools.reduce(jnp.maximum, sides)
    shares = [jnp.exp(side - highest) for side in sides]
    whole = sum(shares)
    shares = [share / whole for share in shares]
    for head in range(HEADS):
        span = slice(head * HEAD_DIM, (head + 1) * HEAD_DIM)
        merged = sum(
            text_back[side, :, span].astype(jnp.float32) * shares[side][:, head : head + 1]
            for side in range(HALVES)
        )
        text_out[0, :, span] = merged.astype(jnp.bfloat16)

    kept[7].wait()
    for copy in self_return:
        copy.wait_recv()
    for copy in text_in + self_in + text_return + self_return:
        copy.wait_send()


def carry(*refs):
    sources, targets, held, sem = refs[0:2], refs[2:4], refs[4:6], refs[6]
    steps = []
    for n in range(2):
        steps.append(pltpu.make_async_copy(sources[n], held[n], sem.at[0, n]))
        steps[n].start()
    ends = []
    for n in range(2):
        steps[n].wait()
        ends.append(pltpu.make_async_copy(held[n], targets[n], sem.at[1, n]))
        ends[n].start()
    for end in ends:
        end.wait()


def fused_shards(self_queries, self_keys, self_values, text_queries, text_kv, text_len):
    count = lax.axis_size("seq")
    rows, channels = self_queries.shape[1:]
    context_rows = text_kv.shape[2]
    ring = count // HALVES
    self_span, text_span = channels // count, channels // ring
    in_place = pl.BlockSpec(memory_space=pl.ANY)
    bf16, f32 = jnp.bfloat16, jnp.float32
    out = jax.ShapeDtypeStruct((1, rows, channels), bf16)
    results = pl.pallas_call(
        functools.partial(fused, count),
        out_shape=(out, out),
        in_specs=[in_place] * 5 + [pl.BlockSpec(memory_space=pltpu.SMEM)],
        out_specs=(in_place, pl.BlockSpec(memory_space=pltpu.VMEM)),
        scratch_shapes=[
            pltpu.VMEM((count, rows, self_span), bf16),
            pltpu.VMEM((count, rows, self_span), bf16),
            pltpu.VMEM((count, rows, self_span), bf16),
            pltpu.VMEM((count, rows, text_span), bf16),
            pltpu.VMEM((ring, 2, context_rows, text_span), bf16),
            pltpu.VMEM((count, rows, self_span), bf16),
            pltpu.VMEM((count, rows, text_span), bf16),
            pltpu.VMEM((text_span // HEAD_DIM, count * rows), f32),
            pltpu.VMEM((HALVES, rows, channels), bf16),
            pltpu.VMEM((count, text_span // HEAD_DIM, count * rows), f32),
            pltpu.VMEM((count * rows, HALVES * HEADS), f32),
            pltpu.SemaphoreType.DMA((8, count)),
            pltpu.SemaphoreType.DMA((8, count)),
            pltpu.SemaphoreType.DMA((8,)),
        ],
        compiler_params=pltpu.CompilerParams(collective_id=0, has_side_effects=True),
        name="attention",
    )(self_queries, self_keys, self_values, text_queries, text_kv, text_len)
    return pl.pallas_call(
        carry,
        out_shape=(out, out),
        in_specs=[in_place] * 2,
        out_specs=(in_place, in_place),
        scratch_shapes=[
            pltpu.VMEM((1, rows, channels), bf16),
            pltpu.VMEM((1, rows, channels), bf16),
            pltpu.SemaphoreType.DMA((2, 2)),
        ],
        name="carry",
    )(*results)


def solution(mesh):
    count = mesh.shape["seq"]
    fits = count % HALVES == 0 and HEADS % count == 0
    return jax.shard_map(
        fused_shards if fits else shards,
        mesh=mesh,
        in_specs=(
            P("enc", ("groups", "seq"), None),
            P("enc", ("groups", "seq"), None),
            P("enc", ("groups", "seq"), None),
            P("enc", ("groups", "seq"), None),
            P("enc", None, ("groups", "seq"), None),
            P("groups"),
        ),
        out_specs=(P("enc", ("groups", "seq"), None), P("enc", ("groups", "seq"), None)),
        check_vma=False,
    )
```

profile of v0, /device:TPU:0, one launch (start us, length us, event | category | flops | bytes accessed | tf_op | source)
XLA Modules:
  0.0 41.9 jit_solution(5161089833428148231)
XLA Ops:
  0.6 39.7 %attention.1 = (bf16[1,16,4096]{2,1,0:T(8,128)(2,1)}, bf16[1,16,4096]{2,1,0:T(8,128)(2,1)}) custom-call(bf16[1,16,4096]{2,1,0:T(8,128)(2,1)} %self_q.1, bf16[1,16,4096]{2,1,0:T(8,128)(2,1)} %self_k.1, bf16[1,16,4096]{2,1,0:T(8,128)(2,1)} %self_v.1, bf16[1,16,4096]{2,1,0:T(8,128)(2,1)} %text_q.1, bf16[1,2,64,4096]{3,2,1,0:T(8,128)(2,1)} %text_kv.1, s32[2]{0:T(128)} %text_len.1), custom_call_target="tpu_custom_call" | custom-call | tf_op jit(solution)/shard_map/attention/pallas_call | solution.py:354
  40.3 1.7 %carry.1 = (bf16[1,16,4096]{2,1,0:T(8,128)(2,1)}, bf16[1,16,4096]{2,1,0:T(8,128)(2,1)}) custom-call(bf16[1,16,4096]{2,1,0:T(8,128)(2,1)} %get-tuple-element.4.refs_0_, bf16[1,16,4096]{2,1,0:T(8,128)(2,1)} %get-tuple-element.5.refs_1_), custom_call_target="tpu_custom_call" | custom-call | tf_op jit(solution)/shard_map/carry/pallas_call | solution.py:378
where the time goes:
time: 42.1 us; the launch traced here: 41.9 us
  Pallas kernels  41.3 us (98%)
  between operations  0.64 us (2%)
    pallas_call x1, Pallas kernels, fused_shards(): pl.pallas_call(functools.partial(fused, count), out_shape=(out, out), in_...  39.7 us
    pallas_call x1, Pallas kernels, fused_shards(): pl.pallas_call(carry, out_shape=(out, out), in_specs=[in_place] * 2, out_...  1.66 us

commit v1 on v0

v1 whole, which is shorter than its diff:
```python
import functools
import math

import jax
import jax.numpy as jnp
from jax import lax
from jax.experimental import pallas as pl
from jax.experimental.pallas import tpu as pltpu
from jax.sharding import PartitionSpec as P

HEADS = 32
HEAD_DIM = 128


def absorb(run_state, queries, key_rows, value_rows, live_mask):
    running_max, row_total, weighted_sum = run_state
    scores = jnp.einsum(
        "qpd,kpd->pqk", queries, key_rows, preferred_element_type=jnp.float32
    ) / math.sqrt(HEAD_DIM)
    scores = jnp.where(live_mask[None, None, :], scores, -1e30)
    new_max = jnp.maximum(running_max, jnp.max(scores, axis=2))
    weights = jnp.where(live_mask[None, None, :], jnp.exp(scores - new_max[:, :, None]), 0.0)
    factor = jnp.exp(running_max - new_max)
    row_total = row_total * factor + jnp.sum(weights, axis=2)
    weighted_sum = weighted_sum * factor[:, :, None] + jnp.einsum(
        "pqk,kpd->pqd", weights.astype(jnp.bfloat16), value_rows, preferred_element_type=jnp.float32
    )
    return (new_max, row_total, weighted_sum)


def empty_state(head_count, query_count):
    return (
        jnp.full((head_count, query_count), -1e30, jnp.float32),
        jnp.zeros((head_count, query_count), jnp.float32),
        jnp.zeros((head_count, query_count, HEAD_DIM), jnp.float32),
    )


def finish(run_state):
    running_max, row_total, weighted_sum = run_state
    return (weighted_sum / row_total[:, :, None]).transpose(1, 0, 2).astype(jnp.bfloat16)


def block_attention(queries, key_rows, value_rows, live_mask):
    query_total, heads_here, head_width = queries.shape
    key_total = key_rows.shape[0]
    key_block = 1024 if key_total % 1024 == 0 else key_total
    query_block = 512 if query_total % 512 == 0 else query_total
    key_blocks = key_rows.reshape(key_total // key_block, key_block, heads_here, head_width)
    value_blocks = value_rows.reshape(key_total // key_block, key_block, heads_here, head_width)
    live_blocks = live_mask.reshape(key_total // key_block, key_block)

    def one_block(query_piece):

        def absorb_block(run_state, pieces):
            return (absorb(run_state, query_piece, pieces[0], pieces[1], pieces[2]), None)

        final_state, unused = lax.scan(
            absorb_block,
            empty_state(heads_here, query_block),
            (key_blocks, value_blocks, live_blocks),
        )
        return finish(final_state)

    blended = lax.map(
        one_block, queries.reshape(query_total // query_block, query_block, heads_here, head_width)
    )
    return blended.reshape(query_total, heads_here, head_width)


def shards(self_queries, self_keys, self_values, text_queries, text_kv, text_len):
    token_rows = self_queries.shape[1]
    channel_count = self_queries.shape[2]
    seq_count = lax.axis_size("seq")
    quarter_count = max(seq_count // HEADS, 1)
    heads_here = max(HEADS // seq_count, 1)
    group_count = HEADS // heads_here
    head_span = heads_here * HEAD_DIM
    share_rows = token_rows // quarter_count
    query_total = share_rows * seq_count
    branch = lax.axis_index("enc")
    length = lax.dynamic_index_in_dim(text_len, branch, 0, keepdims=False)

    def head_view(tensor):
        return tensor.reshape(1, share_rows, seq_count, head_span)

    def repeated(tensor):
        spread = jnp.broadcast_to(
            tensor.reshape(1, token_rows, 1, group_count, head_span),
            (1, token_rows, quarter_count, group_count, head_span),
        )
        return spread.reshape(1, token_rows, seq_count, head_span)

    head_queries, head_keys, head_values = (
        lax.all_to_all(head_view(self_queries), "seq", split_axis=2, concat_axis=1, tiled=True),
        lax.all_to_all(repeated(self_keys), "seq", split_axis=2, concat_axis=1, tiled=True),
        lax.all_to_all(repeated(self_values), "seq", split_axis=2, concat_axis=1, tiled=True),
    )
    key_rows = head_keys.reshape(-1, heads_here, HEAD_DIM)
    value_rows = head_values.reshape(-1, heads_here, HEAD_DIM)
    query_rows = head_queries.reshape(query_total, heads_here, HEAD_DIM)
    every_key = jnp.ones((key_rows.shape[0],), jnp.bool_)
    self_heads = block_attention(query_rows, key_rows, value_rows, every_key)
    head_text_queries = lax.all_to_all(
        head_view(text_queries), "seq", split_axis=2, concat_axis=1, tiled=True
    )
    context_rows = text_kv.shape[2]
    spread = jnp.broadcast_to(
        text_kv.reshape(1, 2, context_rows, 1, group_count, head_span),
        (1, 2, context_rows, quarter_count, group_count, head_span),
    )
    head_context = lax.all_to_all(
        spread.reshape(1, 2, context_rows, seq_count, head_span),
        "seq",
        split_axis=3,
        concat_axis=2,
        tiled=True,
    )
    text_total = head_context.shape[2]
    context_keys = head_context[0, 0].reshape(text_total, heads_here, HEAD_DIM)
    context_values = head_context[0, 1].reshape(text_total, heads_here, HEAD_DIM)
    live_mask = jnp.arange(text_total, dtype=jnp.int32) < length
    text_heads = block_attention(
        head_text_queries.reshape(query_total, heads_here, HEAD_DIM),
        context_keys,
        context_values,
        live_mask,
    )
    self_view = self_heads.reshape(1, seq_count, share_rows, 1, head_span)
    text_view = text_heads.reshape(1, seq_count, share_rows, 1, head_span)
    self_back, text_back = (
        lax.all_to_all(self_view, "seq", split_axis=1, concat_axis=3, tiled=True),
        lax.all_to_all(text_view, "seq", split_axis=1, concat_axis=3, tiled=True),
    )
    self_mixed = self_back.reshape(1, token_rows, channel_count)
    text_mixed = text_back.reshape(1, token_rows, channel_count)
    return (self_mixed, text_mixed)


COLUMNS = 2
HALVES = 2
PLACES = 4
CHUNKS = 4
SENDS = (
    "query",
    "relay",
    "context",
    "self",
    "self_return",
    "near",
    "near_stat",
    "inbound",
    "inbound_stat",
    "joined",
    "joined_stat",
)
EARLY_OUTER, EARLY_INNER, LATER_INNER, LATE = (2, 4, 6), (6,), (2, 4), (7, 5, 3, 1)
ODD_AFTER = 0
JOINS = ((), (), (0,), (1,), (2, 3))
MESH = pl.DeviceIdType.MESH
FAR = -1e30


def attend(queries, key_rows, value_rows, live):
    scores = lax.dot_general(
        queries, key_rows, (((1,), (1,)), ((), ())), preferred_element_type=jnp.float32
    ) * (1.0 / math.sqrt(HEAD_DIM))
    if live is not None:
        scores = jnp.where(live, scores, FAR)
    top = jnp.max(scores, axis=1, keepdims=True)
    weights = jnp.exp(scores - top)
    if live is not None:
        weights = jnp.where(live, weights, 0.0)
    total = jnp.sum(weights, axis=1, keepdims=True)
    mixed = jnp.dot(weights.astype(jnp.bfloat16), value_rows, preferred_element_type=jnp.float32)
    return mixed, top, total


def fused(
    count,
    self_q,
    self_k,
    self_v,
    text_q,
    text_kv,
    text_len,
    self_out,
    text_back,
    stat_back,
    own,
    self_part,
    text_rows,
    context,
    text_part,
    inbound,
    joined,
    stat_part,
    stat_pack,
    stat_in,
    stat_join,
    stat_sum,
    query_recv,
    context_recv,
    inbound_recv,
    final_recv,
    sends,
    local_sem,
):
    me = lax.axis_index("seq")
    branch = lax.axis_index("enc")
    place, column = lax.div(me, COLUMNS), lax.rem(me, COLUMNS)
    half = lax.div(place, PLACES // HALVES)
    span = count // HALVES
    inner = lax.rem(place, 2) + half == 1
    outer = lax.rem(place, 2) + half != 1
    beside = COLUMNS * place + 1 - column
    near_place = place + 1 - 2 * lax.rem(place, 2)
    near, near_beside = COLUMNS * near_place + column, COLUMNS * near_place + 1 - column
    inner_there, outer_there = 2 - half, (PLACES - 1) * (1 - half)
    across = COLUMNS * inner_there + column
    there = (1 - half) * span
    rows = self_q.shape[1]
    query_total = count * rows
    context_rows = text_kv.shape[2]
    key_total = COLUMNS * context_rows
    self_span = own.shape[2]
    text_span = text_rows.shape[2]
    self_heads, text_heads = self_span // HEAD_DIM, text_span // HEAD_DIM
    chunk_heads = text_heads // CHUNKS
    chunk_span = chunk_heads * HEAD_DIM
    send_of = {name: sends.at[n] for n, name in enumerate(SENDS)}

    def self_cols(device):
        return pl.ds(pl.multiple_of(device * self_span, self_span), self_span)

    def text_cols(side):
        return pl.ds(pl.multiple_of(side * text_span, text_span), text_span)

    def part_cols(side, chunk, width=1):
        return pl.ds(pl.multiple_of(side * text_span + chunk * chunk_span, chunk_span), width * chunk_span)

    def piece(chunk, width=1):
        return pl.ds(chunk * chunk_span, width * chunk_span)

    def remote(source, target, kind, recv, device):
        return pltpu.make_async_remote_copy(
            src_ref=source,
            dst_ref=target,
            send_sem=send_of[kind],
            recv_sem=recv,
            device_id={"seq": device},
            device_id_type=MESH,
        )

    def take(ref, sem):
        pltpu.make_async_copy(ref, ref, sem).wait()

    def start(copies):
        for copy in copies:
            copy.start()

    def mirror(bits):
        far_place = (
            place,
            near_place,
            lax.rem(place + 2, PLACES),
            PLACES - 1 - place,
        )[bits // 2]
        return COLUMNS * far_place + (column if bits % 2 == 0 else 1 - column)

    kept_rows = pltpu.make_async_copy(text_q.at[0, :, text_cols(column)], text_rows.at[me], local_sem.at[0])
    kept_context = pltpu.make_async_copy(
        text_kv.at[0, :, :, text_cols(column)], context.at[column], local_sem.at[1]
    )
    kept_rows.start()
    kept_context.start()
    for kind, source in enumerate((self_q, self_k, self_v)):
        pltpu.make_async_copy(
            source.at[0, :, self_cols(me)], own.at[kind * count + me], local_sem.at[2]
        ).start()

    barrier = pltpu.get_barrier_semaphore()
    for step in range(1, count):
        pl.semaphore_signal(
            barrier, inc=1, device_id={"seq": lax.rem(me + step, count)}, device_id_type=MESH
        )
    with jax.named_scope("entry"):
        pl.semaphore_wait(barrier, count - 1)

    def held(origin, chunk):
        return text_rows.at[origin, :, piece(chunk)]

    def query_copy(kind, slot, chunk, source, origin, device):
        return remote(source, held(origin, chunk), kind, query_recv.at[slot, chunk], device)

    origins = [
        COLUMNS * inner_there + column,
        COLUMNS * outer_there + column,
        COLUMNS * inner_there + 1 - column,
        COLUMNS * outer_there + 1 - column,
    ]
    first = 2 + lax.rem(lax.rem(place, 2) + half + 1, 2)
    for chunk in range(CHUNKS):
        query_copy(
            "query", 0, chunk, text_q.at[0, :, part_cols(1 - column, chunk)], me, beside
        ).start()
    for chunk in range(CHUNKS):
        mine = text_q.at[0, :, part_cols(column, chunk)]
        query_copy("query", first, chunk, mine, me, across).start()
        query_copy("query", 1, chunk, mine, me, near).start()
    for chunk in range(CHUNKS):
        remote(
            text_kv.at[0, :, :, part_cols(1 - column, chunk)],
            context.at[column, :, :, piece(chunk)],
            "context",
            context_recv.at[chunk],
            beside,
        ).start()
    for chunk in range(CHUNKS):
        with jax.named_scope(f"q_beside{chunk}"):
            take(held(beside, chunk), query_recv.at[0, chunk])
        query_copy("query", first + 2, chunk, held(beside, chunk), beside, across).start()
        query_copy("query", 1, chunk, held(beside, chunk), beside, near).start()

    def start_self(bits):
        to = mirror(bits)
        for kind, source in enumerate((self_q, self_k, self_v)):
            remote(
                source.at[0, :, self_cols(to)], own.at[kind * count + me], "self", final_recv.at[3], to
            ).start()

    def far_waits(chunk):
        for n, origin in enumerate(origins):
            with jax.named_scope(f"q_far{chunk}{n}"):
                take(held(origin, chunk), query_recv.at[2 + n, chunk])
            yield n, origin

    @pl.when(outer)
    def _():
        for bits in EARLY_OUTER:
            start_self(bits)

    @pl.when(inner)
    def _():
        for bits in EARLY_INNER:
            start_self(bits)
        for chunk in range(CHUNKS):
            for n, origin in far_waits(chunk):
                query_copy("relay", 2 + n, chunk, held(origin, chunk), origin, near).start()
        for bits in LATER_INNER:
            start_self(bits)

    kept_rows.wait()

    length = text_len[branch]
    live = place * key_total + lax.broadcasted_iota(jnp.int32, (1, key_total), 1) < length
    lane = lax.broadcasted_iota(jnp.int32, (query_total, HEAD_DIM), 1)
    short_lane = lax.broadcasted_iota(jnp.int32, (rows, HEAD_DIM), 1)

    def gathered():
        packed = jnp.zeros((rows, HEAD_DIM), jnp.float32)
        for n in range(span):
            moved = stat_part[there + n]
            if n:
                moved = pltpu.roll(moved, n * text_heads, 1)
            packed = jnp.where(lax.div(short_lane, text_heads) == n, moved, packed)
        return packed

    def join(chunk):
        with jax.named_scope(f"inb{chunk}"):
            take(stat_in.at[chunk], inbound_recv.at[1, chunk])
            take(inbound.at[:, :, piece(chunk)], inbound_recv.at[0, chunk])
        sides = [gathered(), stat_in[chunk]]
        highest = jnp.maximum(*sides)
        shares = [jnp.exp(side - highest) for side in sides]
        whole = shares[0] + shares[1]
        shares = [share / whole for share in shares]
        ours = lax.div(lax.rem(short_lane, text_heads), chunk_heads) == chunk
        stat_sum[...] = jnp.where(ours, highest + jnp.log(whole), stat_sum[...])
        for n in range(span):
            for head in range(chunk * chunk_heads, (chunk + 1) * chunk_heads):
                cols = slice(head * HEAD_DIM, (head + 1) * HEAD_DIM)
                at = n * text_heads + head
                merged = (
                    text_part[there + n, :, cols].astype(jnp.float32) * shares[0][:, at : at + 1]
                    + inbound[n, :, cols].astype(jnp.float32) * shares[1][:, at : at + 1]
                )
                joined[n, :, cols] = merged.astype(jnp.bfloat16)
            remote(
                joined.at[n, :, piece(chunk)],
                text_back.at[HALVES, :, part_cols(column, chunk)],
                "joined",
                final_recv.at[0],
                there + n,
            ).start()
        if chunk == CHUNKS - 1:
            final = stat_sum[...]
            for n in range(span):
                stat_join[n] = pltpu.roll(final, HEAD_DIM - n * text_heads, 1) if n else final
                remote(
                    stat_join.at[n],
                    stat_back.at[HALVES, column],
                    "joined_stat",
                    final_recv.at[1],
                    there + n,
                ).start()

    neighbours = ((0, beside), (1, near), (1, near_beside))
    stats = jnp.full((query_total, HEAD_DIM), FAR, jnp.float32)

    @pl.when(inner)
    def _():
        stat_sum[...] = jnp.zeros_like(stat_sum)

    kept_context.wait()
    for chunk in range(CHUNKS):

        @pl.when(outer)
        def _(chunk=chunk):
            for _n in far_waits(chunk):
                pass

        with jax.named_scope(f"q_near{chunk}"):
            take(text_rows.at[pl.ds(0, 2), :, piece(chunk)], query_recv.at[1, chunk])
        with jax.named_scope(f"kv{chunk}"):
            take(context.at[0, :, :, piece(chunk)], context_recv.at[chunk])
        for head in range(chunk * chunk_heads, (chunk + 1) * chunk_heads):
            cols = slice(head * HEAD_DIM, (head + 1) * HEAD_DIM)
            mixed, top, total = attend(
                text_rows[:, :, cols].reshape(query_total, HEAD_DIM),
                context[:, 0, :, cols].reshape(key_total, HEAD_DIM),
                context[:, 1, :, cols].reshape(key_total, HEAD_DIM),
                live,
            )
            safe = jnp.where(total > 0.0, total, 1.0)
            weight = jnp.where(total > 0.0, top + jnp.log(safe), FAR)
            text_part[:, :, cols] = (mixed / safe).astype(jnp.bfloat16).reshape(count, rows, HEAD_DIM)
            stats = jnp.where(lane == head, weight, stats)
        stat_part[...] = stats.reshape(count, rows, HEAD_DIM)

        @pl.when(outer)
        def _(chunk=chunk):
            stat_pack[chunk] = gathered()
            remote(
                stat_pack.at[chunk], stat_in.at[chunk], "inbound_stat", inbound_recv.at[1, chunk], near
            ).start()
            remote(
                text_part.at[pl.ds(there, span), :, piece(chunk)],
                inbound.at[:, :, piece(chunk)],
                "inbound",
                inbound_recv.at[0, chunk],
                near,
            ).start()

        if chunk == ODD_AFTER:
            for bits in LATE:
                start_self(bits)
        if chunk % 2 == 1:
            for slot, device in neighbours:
                remote(
                    text_part.at[device, :, piece(chunk - 1, 2)],
                    text_back.at[slot, :, part_cols(column, chunk - 1, 2)],
                    "near",
                    final_recv.at[0],
                    device,
                ).start()
        for ready in JOINS[chunk]:

            @pl.when(inner)
            def _(ready=ready):
                join(ready)

    for slot, device in neighbours:
        remote(
            stat_part.at[device], stat_back.at[slot, column], "near_stat", final_recv.at[1], device
        ).start()
    kept_part = pltpu.make_async_copy(text_part.at[me], text_back.at[0, :, text_cols(column)], local_sem.at[0])
    kept_stat = pltpu.make_async_copy(stat_part.at[me], stat_back.at[0, column], local_sem.at[1])
    kept_part.start()
    kept_stat.start()

    take(own.at[pl.ds(0, 3)], local_sem.at[2])
    with jax.named_scope("self"):
        take(own.at[pl.ds(0, 3 * (count - 1))], final_recv.at[3])
    for head in range(self_heads):
        cols = slice(head * HEAD_DIM, (head + 1) * HEAD_DIM)
        mixed, top, total = attend(
            own[0:count, :, cols].reshape(query_total, HEAD_DIM),
            own[count : 2 * count, :, cols].reshape(query_total, HEAD_DIM),
            own[2 * count : 3 * count, :, cols].reshape(query_total, HEAD_DIM),
            None,
        )
        self_part[:, :, cols] = (mixed / total).astype(jnp.bfloat16).reshape(count, rows, HEAD_DIM)
    kept_self = pltpu.make_async_copy(self_part.at[me], self_out.at[0, :, self_cols(me)], local_sem.at[2])
    kept_self.start()
    for bits in (6, 7, 4, 5, 2, 3, 1):
        to = mirror(bits)
        remote(
            self_part.at[to], self_out.at[0, :, self_cols(me)], "self_return", final_recv.at[2], to
        ).start()
    for ready in JOINS[CHUNKS]:

        @pl.when(inner)
        def _(ready=ready):
            join(ready)

    kept_part.wait()
    kept_stat.wait()
    kept_self.wait()
    with jax.named_scope("back"):
        take(text_part.at[pl.ds(0, 3 + COLUMNS)], final_recv.at[0])
    with jax.named_scope("back_stat"):
        take(stat_part.at[pl.ds(0, 3 + COLUMNS)], final_recv.at[1])
    with jax.named_scope("self_out"):
        take(self_part.at[pl.ds(0, count - 1)], final_recv.at[2])
    with jax.named_scope("sends"):
        take(text_rows.at[pl.ds(0, 5)], send_of["query"])
        take(context.at[0], send_of["context"])
        take(own.at[pl.ds(0, 3 * (count - 1))], send_of["self"])
        take(self_part.at[pl.ds(0, count - 1)], send_of["self_return"])
        take(text_part.at[pl.ds(0, 3)], send_of["near"])
        take(stat_part.at[pl.ds(0, 3)], send_of["near_stat"])

    @pl.when(outer)
    def _():
        take(inbound, send_of["inbound"])
        take(stat_pack, send_of["inbound_stat"])

    @pl.when(inner)
    def _():
        take(text_rows.at[pl.ds(0, span)], send_of["relay"])
        take(joined, send_of["joined"])
        take(stat_join, send_of["joined_stat"])


def settle(self_in, text_in, stat_in, self_out, text_out, self_held, text_held, stat_held, mixed, in_sem, out_sem):
    channels = text_in.shape[2]
    text_span = channels // COLUMNS
    arrivals = [
        pltpu.make_async_copy(stat_in, stat_held, in_sem.at[0]),
        pltpu.make_async_copy(self_in, self_held, in_sem.at[1]),
    ]
    for side in range(COLUMNS):
        piece = pl.ds(side * text_span, text_span)
        arrivals.append(
            pltpu.make_async_copy(text_in.at[:, :, piece], text_held.at[:, :, piece], in_sem.at[2 + side])
        )
    for copy in arrivals:
        copy.start()
    leaving = [pltpu.make_async_copy(self_held, self_out, out_sem.at[0])]
    arrivals[0].wait()
    arrivals[1].wait()
    leaving[0].start()
    for side in range(COLUMNS):
        sides = [stat_held[n, side] for n in range(HALVES + 1)]
        highest = functools.reduce(jnp.maximum, sides)
        shares = [jnp.exp(each - highest) for each in sides]
        whole = sum(shares)
        shares = [share / whole for share in shares]
        arrivals[2 + side].wait()
        for head in range(text_span // HEAD_DIM):
            cols = slice(side * text_span + head * HEAD_DIM, side * text_span + (head + 1) * HEAD_DIM)
            merged = sum(
                text_held[n, :, cols].astype(jnp.float32) * shares[n][:, head : head + 1]
                for n in range(HALVES + 1)
            )
            mixed[0, :, cols] = merged.astype(jnp.bfloat16)
        piece = pl.ds(side * text_span, text_span)
        leaving.append(
            pltpu.make_async_copy(mixed.at[:, :, piece], text_out.at[:, :, piece], out_sem.at[1 + side])
        )
        leaving[1 + side].start()
    for copy in leaving:
        copy.wait()


def fused_shards(self_queries, self_keys, self_values, text_queries, text_kv, text_len):
    count = lax.axis_size("seq")
    rows, channels = self_queries.shape[1:]
    context_rows = text_kv.shape[2]
    span = count // HALVES
    self_span, text_span = channels // count, channels // COLUMNS
    in_place = pl.BlockSpec(memory_space=pl.ANY)
    bf16, f32 = jnp.bfloat16, jnp.float32
    out = jax.ShapeDtypeStruct((1, rows, channels), bf16)
    dma = pltpu.SemaphoreType.DMA
    results = pl.pallas_call(
        functools.partial(fused, count),
        out_shape=(
            out,
            jax.ShapeDtypeStruct((HALVES + 1, rows, channels), bf16),
            jax.ShapeDtypeStruct((HALVES + 1, COLUMNS, rows, HEAD_DIM), f32),
        ),
        in_specs=[in_place] * 5 + [pl.BlockSpec(memory_space=pltpu.SMEM)],
        out_specs=(in_place, in_place, in_place),
        scratch_shapes=[
            pltpu.VMEM((3 * count, rows, self_span), bf16),
            pltpu.VMEM((count, rows, self_span), bf16),
            pltpu.VMEM((count, rows, text_span), bf16),
            pltpu.VMEM((COLUMNS, 2, context_rows, text_span), bf16),
            pltpu.VMEM((count, rows, text_span), bf16),
            pltpu.VMEM((span, rows, text_span), bf16),
            pltpu.VMEM((span, rows, text_span), bf16),
            pltpu.VMEM((count, rows, HEAD_DIM), f32),
            pltpu.VMEM((CHUNKS, rows, HEAD_DIM), f32),
            pltpu.VMEM((CHUNKS, rows, HEAD_DIM), f32),
            pltpu.VMEM((span, rows, HEAD_DIM), f32),
            pltpu.VMEM((rows, HEAD_DIM), f32),
            dma((2 + span, CHUNKS)),
            dma((CHUNKS,)),
            dma((2, CHUNKS)),
            dma((4,)),
            dma((len(SENDS),)),
            dma((3,)),
        ],
        compiler_params=pltpu.CompilerParams(collective_id=0, has_side_effects=True),
        name="attention",
    )(self_queries, self_keys, self_values, text_queries, text_kv, text_len)
    return pl.pallas_call(
        settle,
        out_shape=(out, out),
        in_specs=[in_place] * 3,
        out_specs=(in_place, in_place),
        scratch_shapes=[
            pltpu.VMEM((1, rows, channels), bf16),
            pltpu.VMEM((HALVES + 1, rows, channels), bf16),
            pltpu.VMEM((HALVES + 1, COLUMNS, rows, HEAD_DIM), f32),
            pltpu.VMEM((1, rows, channels), bf16),
            dma((2 + COLUMNS,)),
            dma((1 + COLUMNS,)),
        ],
        name="settle",
    )(*results)


def solution(mesh):
    count = mesh.shape["seq"]
    fits = count == COLUMNS * PLACES and HEADS % count == 0
    return jax.shard_map(
        fused_shards if fits else shards,
        mesh=mesh,
        in_specs=(
            P("enc", ("groups", "seq"), None),
            P("enc", ("groups", "seq"), None),
            P("enc", ("groups", "seq"), None),
            P("enc", ("groups", "seq"), None),
            P("enc", None, ("groups", "seq"), None),
            P("groups"),
        ),
        out_specs=(P("enc", ("groups", "seq"), None), P("enc", ("groups", "seq"), None)),
        check_vma=False,
    )
```

time: 42.1 us -> 37.9 us (0.900)
  Pallas kernels: 41.3 us -> 37.1 us
    pallas_call x2, Pallas kernels: 41.3 us -> 37.1 us  [the longest x1 35 us: fused_shards(): pl.pallas_call(functools.partial(fused, count), out_shape=(out, jax.Shape...]
where the time goes in v1:
time: 37.9 us; the launch traced here: 37.7 us
  Pallas kernels  37.1 us (98%)
  between operations  0.64 us (2%)
    pallas_call x1, Pallas kernels, fused_shards(): pl.pallas_call(functools.partial(fused, count), out_shape=(out, jax.Shape...  35 us
    pallas_call x1, Pallas kernels, fused_shards(): pl.pallas_call(settle, out_shape=(out, out), in_specs=[in_place] * 3, out...  2.1 us

profile of v1, /device:TPU:0, one launch (start us, length us, event | category | flops | bytes accessed | tf_op | source)
XLA Modules:
  0.0 37.7 jit_solution(2653257512180227666)
XLA Ops:
  0.6 35.0 %attention.1 = (bf16[1,16,4096]{2,1,0:T(8,128)(2,1)}, bf16[3,16,4096]{2,1,0:T(8,128)(2,1)}, f32[3,2,16,128]{3,2,1,0:T(8,128)}) custom-call(bf16[1,16,4096]{2,1,0:T(8,128)(2,1)} %self_q.1, bf16[1,16,4096]{2,1,0:T(8,128)(2,1)} %self_k.1, bf16[1,16,4096]{2,1,0:T(8,128)(2,1)} %self_v.1, bf16[1,16,4096]{2,1,0:T(8,128)(2,1)} %text_q.1, ...), custom_call_target="tpu_custom_call" | custom-call | tf_op jit(solution)/shard_map/attention/pallas_call | solution.py:587
  35.6 2.1 %settle.1 = (bf16[1,16,4096]{2,1,0:T(8,128)(2,1)}, bf16[1,16,4096]{2,1,0:T(8,128)(2,1)}) custom-call(bf16[1,16,4096]{2,1,0:T(8,128)(2,1)} %get-tuple-element.5.self_in, bf16[3,16,4096]{2,1,0:T(8,128)(2,1)} %get-tuple-element.6.text_in, f32[3,2,16,128]{3,2,1,0:T(8,128)} %get-tuple-element.7.stat_in), custom_call_target="tpu_custom_call" | custom-call | tf_op jit(solution)/shard_map/settle/pallas_call | solution.py:619

commit v2 on v1

--- a/solution.py
+++ b/solution.py
@@ -141,6 +141,7 @@
 HALVES = 2
 PLACES = 4
 CHUNKS = 4
+GRANT = 12 * 1024 * 1024
 SENDS = (
     "query",
     "relay",
@@ -154,26 +155,25 @@
     "joined",
     "joined_stat",
 )
-EARLY_OUTER, EARLY_INNER, LATER_INNER, LATE = (2, 4, 6), (6,), (2, 4), (7, 5, 3, 1)
-ODD_AFTER = 0
-JOINS = ((), (), (0,), (1,), (2, 3))
+OUTER = ('b2', 'b4', 'b6', 'c0', 'b7', 'b5', 'b3', 'b1', 'c1', 'c2', 'c3', 'n01', 'n23', 't', 's')
+INNER = ('b6', 'r', 'b2', 'b4', 'c0', 'b7', 'b5', 'b3', 'b1', 'c1', 'n01', 'c2', 'j0', 'c3', 'n23', 'j1', 't', 's', 'j2', 'j3')
+LATER = tuple(sorted(int(step[1]) for step in OUTER if step[0] == "x"))
 MESH = pl.DeviceIdType.MESH
 FAR = -1e30
+SCALE = math.log2(math.e) / math.sqrt(HEAD_DIM)
 
 
 def attend(queries, key_rows, value_rows, live):
     scores = lax.dot_general(
         queries, key_rows, (((1,), (1,)), ((), ())), preferred_element_type=jnp.float32
-    ) * (1.0 / math.sqrt(HEAD_DIM))
+    )
     if live is not None:
         scores = jnp.where(live, scores, FAR)
     top = jnp.max(scores, axis=1, keepdims=True)
-    weights = jnp.exp(scores - top)
-    if live is not None:
-        weights = jnp.where(live, weights, 0.0)
+    weights = jnp.exp2((scores - top) * SCALE)
     total = jnp.sum(weights, axis=1, keepdims=True)
     mixed = jnp.dot(weights.astype(jnp.bfloat16), value_rows, preferred_element_type=jnp.float32)
-    return mixed, top, total
+    return mixed / total, top, total
 
 
 def fused(
@@ -187,11 +187,13 @@
     self_out,
     text_back,
     stat_back,
+    own_back,
     own,
     self_part,
     text_rows,
     context,
     text_part,
+    text_full,
     inbound,
     joined,
     stat_part,
@@ -199,6 +201,7 @@
     stat_in,
     stat_join,
     stat_sum,
+    live_len,
     query_recv,
     context_recv,
     inbound_recv,
@@ -268,10 +271,17 @@
         )[bits // 2]
         return COLUMNS * far_place + (column if bits % 2 == 0 else 1 - column)
 
+    barrier = pltpu.get_barrier_semaphore()
+    for step in range(1, count):
+        pl.semaphore_signal(
+            barrier, inc=1, device_id={"seq": lax.rem(me + step, count)}, device_id_type=MESH
+        )
+    kept_len = pltpu.make_async_copy(text_len, live_len, local_sem.at[3])
     kept_rows = pltpu.make_async_copy(text_q.at[0, :, text_cols(column)], text_rows.at[me], local_sem.at[0])
     kept_context = pltpu.make_async_copy(
         text_kv.at[0, :, :, text_cols(column)], context.at[column], local_sem.at[1]
     )
+    kept_len.start()
     kept_rows.start()
     kept_context.start()
     for kind, source in enumerate((self_q, self_k, self_v)):
@@ -279,11 +289,6 @@
             source.at[0, :, self_cols(me)], own.at[kind * count + me], local_sem.at[2]
         ).start()
 
-    barrier = pltpu.get_barrier_semaphore()
-    for step in range(1, count):
-        pl.semaphore_signal(
-            barrier, inc=1, device_id={"seq": lax.rem(me + step, count)}, device_id_type=MESH
-        )
     with jax.named_scope("entry"):
         pl.semaphore_wait(barrier, count - 1)
 
@@ -308,7 +313,7 @@
         mine = text_q.at[0, :, part_cols(column, chunk)]
         query_copy("query", first, chunk, mine, me, across).start()
         query_copy("query", 1, chunk, mine, me, near).start()
-    for chunk in range(CHUNKS):
+    def context_send(chunk):
         remote(
             text_kv.at[0, :, :, part_cols(1 - column, chunk)],
             context.at[column, :, :, piece(chunk)],
@@ -316,6 +321,16 @@
             context_recv.at[chunk],
             beside,
         ).start()
+
+    for chunk in range(CHUNKS):
+        if chunk not in LATER:
+            context_send(chunk)
+
+    @pl.when(branch == 0)
+    def _():
+        for chunk in LATER:
+            context_send(chunk)
+
     for chunk in range(CHUNKS):
         with jax.named_scope(f"q_beside{chunk}"):
             take(held(beside, chunk), query_recv.at[0, chunk])
@@ -335,24 +350,10 @@
                 take(held(origin, chunk), query_recv.at[2 + n, chunk])
             yield n, origin
 
-    @pl.when(outer)
-    def _():
-        for bits in EARLY_OUTER:
-            start_self(bits)
-
-    @pl.when(inner)
-    def _():
-        for bits in EARLY_INNER:
-            start_self(bits)
-        for chunk in range(CHUNKS):
-            for n, origin in far_waits(chunk):
-                query_copy("relay", 2 + n, chunk, held(origin, chunk), origin, near).start()
-        for bits in LATER_INNER:
-            start_self(bits)
-
     kept_rows.wait()
 
-    length = text_len[branch]
+    kept_len.wait()
+    length = live_len[branch]
     live = place * key_total + lax.broadcasted_iota(jnp.int32, (1, key_total), 1) < length
     lane = lax.broadcasted_iota(jnp.int32, (query_total, HEAD_DIM), 1)
     short_lane = lax.broadcasted_iota(jnp.int32, (rows, HEAD_DIM), 1)
@@ -372,17 +373,28 @@
             take(inbound.at[:, :, piece(chunk)], inbound_recv.at[0, chunk])
         sides = [gathered(), stat_in[chunk]]
         highest = jnp.maximum(*sides)
-        shares = [jnp.exp(side - highest) for side in sides]
+        shares = [jnp.exp2(side - highest) for side in sides]
         whole = shares[0] + shares[1]
         shares = [share / whole for share in shares]
         ours = lax.div(lax.rem(short_lane, text_heads), chunk_heads) == chunk
-        stat_sum[...] = jnp.where(ours, highest + jnp.log(whole), stat_sum[...])
+        final = jnp.where(ours, highest + jnp.log2(whole), stat_sum[...])
+        stat_sum[...] = final
+        for n in range(span):
+            if chunk == CHUNKS - 1:
+                stat_join[n] = pltpu.roll(final, HEAD_DIM - n * text_heads, 1) if n else final
+                remote(
+                    stat_join.at[n],
+                    stat_back.at[HALVES, column],
+                    "joined_stat",
+                    final_recv.at[1],
+                    there + n,
+                ).start()
         for n in range(span):
             for head in range(chunk * chunk_heads, (chunk + 1) * chunk_heads):
                 cols = slice(head * HEAD_DIM, (head + 1) * HEAD_DIM)
                 at = n * text_heads + head
                 merged = (
-                    text_part[there + n, :, cols].astype(jnp.float32) * shares[0][:, at : at + 1]
+                    text_full[there + n, :, cols] * shares[0][:, at : at + 1]
                     + inbound[n, :, cols].astype(jnp.float32) * shares[1][:, at : at + 1]
                 )
                 joined[n, :, cols] = merged.astype(jnp.bfloat16)
@@ -393,37 +405,18 @@
                 final_recv.at[0],
                 there + n,
             ).start()
-        if chunk == CHUNKS - 1:
-            final = stat_sum[...]
-            for n in range(span):
-                stat_join[n] = pltpu.roll(final, HEAD_DIM - n * text_heads, 1) if n else final
-                remote(
-                    stat_join.at[n],
-                    stat_back.at[HALVES, column],
-                    "joined_stat",
-                    final_recv.at[1],
-                    there + n,
-                ).start()
 
     neighbours = ((0, beside), (1, near), (1, near_beside))
-    stats = jnp.full((query_total, HEAD_DIM), FAR, jnp.float32)
-
-    @pl.when(inner)
-    def _():
-        stat_sum[...] = jnp.zeros_like(stat_sum)
-
-    kept_context.wait()
-    for chunk in range(CHUNKS):
-
-        @pl.when(outer)
-        def _(chunk=chunk):
+
+    def text_chunk(chunk, role):
+        if role == "outer":
             for _n in far_waits(chunk):
                 pass
-
         with jax.named_scope(f"q_near{chunk}"):
             take(text_rows.at[pl.ds(0, 2), :, piece(chunk)], query_recv.at[1, chunk])
         with jax.named_scope(f"kv{chunk}"):
             take(context.at[0, :, :, piece(chunk)], context_recv.at[chunk])
+        tops, totals = jnp.full((query_total, HEAD_DIM), FAR, jnp.float32), 1.0
         for head in range(chunk * chunk_heads, (chunk + 1) * chunk_heads):
             cols = slice(head * HEAD_DIM, (head + 1) * HEAD_DIM)
             mixed, top, total = attend(
@@ -432,18 +425,12 @@
                 context[:, 1, :, cols].reshape(key_total, HEAD_DIM),
                 live,
             )
-            safe = jnp.where(total > 0.0, total, 1.0)
-            weight = jnp.where(total > 0.0, top + jnp.log(safe), FAR)
-            text_part[:, :, cols] = (mixed / safe).astype(jnp.bfloat16).reshape(count, rows, HEAD_DIM)
-            stats = jnp.where(lane == head, weight, stats)
-        stat_part[...] = stats.reshape(count, rows, HEAD_DIM)
-
-        @pl.when(outer)
-        def _(chunk=chunk):
-            stat_pack[chunk] = gathered()
-            remote(
-                stat_pack.at[chunk], stat_in.at[chunk], "inbound_stat", inbound_recv.at[1, chunk], near
-            ).start()
+            share = mixed.reshape(count, rows, HEAD_DIM)
+            text_full[:, :, cols] = share
+            text_part[:, :, cols] = share.astype(jnp.bfloat16)
+            tops = jnp.where(lane == head, top, tops)
+            totals = jnp.where(lane == head, total, totals)
+        if role == "outer":
             remote(
                 text_part.at[pl.ds(there, span), :, piece(chunk)],
                 inbound.at[:, :, piece(chunk)],
@@ -451,59 +438,93 @@
                 inbound_recv.at[0, chunk],
                 near,
             ).start()
-
-        if chunk == ODD_AFTER:
-            for bits in LATE:
-                start_self(bits)
-        if chunk % 2 == 1:
-            for slot, device in neighbours:
-                remote(
-                    text_part.at[device, :, piece(chunk - 1, 2)],
-                    text_back.at[slot, :, part_cols(column, chunk - 1, 2)],
-                    "near",
-                    final_recv.at[0],
-                    device,
-                ).start()
-        for ready in JOINS[chunk]:
-
-            @pl.when(inner)
-            def _(ready=ready):
-                join(ready)
-
-    for slot, device in neighbours:
-        remote(
-            stat_part.at[device], stat_back.at[slot, column], "near_stat", final_recv.at[1], device
-        ).start()
-    kept_part = pltpu.make_async_copy(text_part.at[me], text_back.at[0, :, text_cols(column)], local_sem.at[0])
+        levels = (tops * SCALE + jnp.log2(totals)).reshape(count, rows, HEAD_DIM)
+        if chunk:
+            before = lax.broadcasted_iota(jnp.int32, (1, 1, HEAD_DIM), 2) < chunk * chunk_heads
+            levels = jnp.where(before, stat_part[...], levels)
+        stat_part[...] = levels
+        if role == "outer":
+            stat_pack[chunk] = gathered()
+            remote(
+                stat_pack.at[chunk], stat_in.at[chunk], "inbound_stat", inbound_recv.at[1, chunk], near
+            ).start()
+
+    def near_send(low, high):
+        for slot, device in neighbours:
+            remote(
+                text_part.at[device, :, piece(low, high + 1 - low)],
+                text_back.at[slot, :, part_cols(column, low, high + 1 - low)],
+                "near",
+                final_recv.at[0],
+                device,
+            ).start()
+
+    def near_stats():
+        for slot, device in neighbours:
+            remote(
+                stat_part.at[device], stat_back.at[slot, column], "near_stat", final_recv.at[1], device
+            ).start()
+
+    def self_attention():
+        take(own.at[pl.ds(0, 3)], local_sem.at[2])
+        with jax.named_scope("self"):
+            take(own.at[pl.ds(0, 3 * (count - 1))], final_recv.at[3])
+        for head in range(self_heads):
+            cols = slice(head * HEAD_DIM, (head + 1) * HEAD_DIM)
+            mixed, _, _ = attend(
+                own[0:count, :, cols].reshape(query_total, HEAD_DIM),
+                own[count : 2 * count, :, cols].reshape(query_total, HEAD_DIM),
+                own[2 * count : 3 * count, :, cols].reshape(query_total, HEAD_DIM),
+                None,
+            )
+            self_part[:, :, cols] = mixed.astype(jnp.bfloat16).reshape(count, rows, HEAD_DIM)
+        for n in range(count - 1):
+            to = n + lax.div(n + count - me, count)
+            remote(
+                self_part.at[to], self_out.at[0, :, self_cols(me)], "self_return", final_recv.at[2], to
+            ).start()
+
+    def relay():
+        for chunk in range(CHUNKS):
+            for n, origin in far_waits(chunk):
+                query_copy("relay", 2 + n, chunk, held(origin, chunk), origin, near).start()
+
+    def run(role, steps):
+        for step in steps:
+            name, _, only = step.partition(".")
+            kind, digits = name[0], [int(digit) for digit in name[1:]]
+            action = {
+                "b": start_self,
+                "x": context_send,
+                "c": functools.partial(text_chunk, role=role),
+                "n": near_send,
+                "j": join,
+                "r": relay,
+                "t": near_stats,
+                "s": self_attention,
+            }[kind]
+            if only:
+                pl.when(branch == int(only))(functools.partial(action, *digits))
+            else:
+                action(*digits)
+
+    kept_context.wait()
+
+    @pl.when(outer)
+    def _():
+        run("outer", OUTER)
+
+    @pl.when(inner)
+    def _():
+        stat_sum[...] = jnp.zeros_like(stat_sum)
+        run("inner", INNER)
+
+    kept_part = pltpu.make_async_copy(text_full.at[me], own_back, local_sem.at[0])
     kept_stat = pltpu.make_async_copy(stat_part.at[me], stat_back.at[0, column], local_sem.at[1])
+    kept_self = pltpu.make_async_copy(self_part.at[me], self_out.at[0, :, self_cols(me)], local_sem.at[2])
     kept_part.start()
     kept_stat.start()
-
-    take(own.at[pl.ds(0, 3)], local_sem.at[2])
-    with jax.named_scope("self"):
-        take(own.at[pl.ds(0, 3 * (count - 1))], final_recv.at[3])
-    for head in range(self_heads):
-        cols = slice(head * HEAD_DIM, (head + 1) * HEAD_DIM)
-        mixed, top, total = attend(
-            own[0:count, :, cols].reshape(query_total, HEAD_DIM),
-            own[count : 2 * count, :, cols].reshape(query_total, HEAD_DIM),
-            own[2 * count : 3 * count, :, cols].reshape(query_total, HEAD_DIM),
-            None,
-        )
-        self_part[:, :, cols] = (mixed / total).astype(jnp.bfloat16).reshape(count, rows, HEAD_DIM)
-    kept_self = pltpu.make_async_copy(self_part.at[me], self_out.at[0, :, self_cols(me)], local_sem.at[2])
     kept_self.start()
-    for bits in (6, 7, 4, 5, 2, 3, 1):
-        to = mirror(bits)
-        remote(
-            self_part.at[to], self_out.at[0, :, self_cols(me)], "self_return", final_recv.at[2], to
-        ).start()
-    for ready in JOINS[CHUNKS]:
-
-        @pl.when(inner)
-        def _(ready=ready):
-            join(ready)
-
     kept_part.wait()
     kept_stat.wait()
     kept_self.wait()
@@ -533,36 +554,27 @@
         take(stat_join, send_of["joined_stat"])
 
 
-def settle(self_in, text_in, stat_in, self_out, text_out, self_held, text_held, stat_held, mixed, in_sem, out_sem):
-    channels = text_in.shape[2]
-    text_span = channels // COLUMNS
-    arrivals = [
-        pltpu.make_async_copy(stat_in, stat_held, in_sem.at[0]),
-        pltpu.make_async_copy(self_in, self_held, in_sem.at[1]),
-    ]
-    for side in range(COLUMNS):
-        piece = pl.ds(side * text_span, text_span)
-        arrivals.append(
-            pltpu.make_async_copy(text_in.at[:, :, piece], text_held.at[:, :, piece], in_sem.at[2 + side])
-        )
-    for copy in arrivals:
-        copy.start()
-    leaving = [pltpu.make_async_copy(self_held, self_out, out_sem.at[0])]
-    arrivals[0].wait()
-    arrivals[1].wait()
+def settle(self_in, text_in, stat_in, own_in, self_out, text_out, mixed, out_sem):
+    column = lax.rem(lax.axis_index("seq"), COLUMNS)
+    text_span = own_in.shape[1]
+    leaving = [pltpu.make_async_copy(self_in, self_out, out_sem.at[0])]
     leaving[0].start()
     for side in range(COLUMNS):
-        sides = [stat_held[n, side] for n in range(HALVES + 1)]
+        sides = [stat_in[n, side] for n in range(HALVES + 1)]
         highest = functools.reduce(jnp.maximum, sides)
-        shares = [jnp.exp(each - highest) for each in sides]
+        shares = [jnp.exp2(each - highest) for each in sides]
         whole = sum(shares)
         shares = [share / whole for share in shares]
-        arrivals[2 + side].wait()
         for head in range(text_span // HEAD_DIM):
             cols = slice(side * text_span + head * HEAD_DIM, side * text_span + (head + 1) * HEAD_DIM)
-            merged = sum(
-                text_held[n, :, cols].astype(jnp.float32) * shares[n][:, head : head + 1]
-                for n in range(HALVES + 1)
+            here = jnp.where(
+                column == side,
+                own_in[:, head * HEAD_DIM : (head + 1) * HEAD_DIM],
+                text_in[0, :, cols].astype(jnp.float32),
+            )
+            merged = here * shares[0][:, head : head + 1] + sum(
+                text_in[n, :, cols].astype(jnp.float32) * shares[n][:, head : head + 1]
+                for n in range(1, HALVES + 1)
             )
             mixed[0, :, cols] = merged.astype(jnp.bfloat16)
         piece = pl.ds(side * text_span, text_span)
@@ -580,6 +592,7 @@
     context_rows = text_kv.shape[2]
     span = count // HALVES
     self_span, text_span = channels // count, channels // COLUMNS
+    operands = (self_queries, self_keys, self_values, text_queries, text_kv, text_len)
     in_place = pl.BlockSpec(memory_space=pl.ANY)
     bf16, f32 = jnp.bfloat16, jnp.float32
     out = jax.ShapeDtypeStruct((1, rows, channels), bf16)
@@ -590,15 +603,17 @@
             out,
             jax.ShapeDtypeStruct((HALVES + 1, rows, channels), bf16),
             jax.ShapeDtypeStruct((HALVES + 1, COLUMNS, rows, HEAD_DIM), f32),
+            jax.ShapeDtypeStruct((rows, text_span), f32),
         ),
-        in_specs=[in_place] * 5 + [pl.BlockSpec(memory_space=pltpu.SMEM)],
-        out_specs=(in_place, in_place, in_place),
+        in_specs=[in_place] * 6,
+        out_specs=(in_place,) * 4,
         scratch_shapes=[
             pltpu.VMEM((3 * count, rows, self_span), bf16),
             pltpu.VMEM((count, rows, self_span), bf16),
             pltpu.VMEM((count, rows, text_span), bf16),
             pltpu.VMEM((COLUMNS, 2, context_rows, text_span), bf16),
             pltpu.VMEM((count, rows, text_span), bf16),
+            pltpu.VMEM((count, rows, text_span), f32),
             pltpu.VMEM((span, rows, text_span), bf16),
             pltpu.VMEM((span, rows, text_span), bf16),
             pltpu.VMEM((count, rows, HEAD_DIM), f32),
@@ -606,29 +621,26 @@
             pltpu.VMEM((CHUNKS, rows, HEAD_DIM), f32),
             pltpu.VMEM((span, rows, HEAD_DIM), f32),
             pltpu.VMEM((rows, HEAD_DIM), f32),
+            pltpu.SMEM(text_len.shape, jnp.int32),
             dma((2 + span, CHUNKS)),
             dma((CHUNKS,)),
             dma((2, CHUNKS)),
             dma((4,)),
             dma((len(SENDS),)),
-            dma((3,)),
+            dma((4,)),
         ],
-        compiler_params=pltpu.CompilerParams(collective_id=0, has_side_effects=True),
+        compiler_params=pltpu.CompilerParams(
+            collective_id=0, has_side_effects=True, vmem_limit_bytes=GRANT
+        ),
         name="attention",
-    )(self_queries, self_keys, self_values, text_queries, text_kv, text_len)
+    )(*[pltpu.with_memory_space_constraint(each, pltpu.HBM) for each in operands])
     return pl.pallas_call(
         settle,
         out_shape=(out, out),
-        in_specs=[in_place] * 3,
+        in_specs=[pl.BlockSpec(memory_space=pltpu.VMEM)] * 4,
         out_specs=(in_place, in_place),
-        scratch_shapes=[
-            pltpu.VMEM((1, rows, channels), bf16),
-            pltpu.VMEM((HALVES + 1, rows, channels), bf16),
-            pltpu.VMEM((HALVES + 1, COLUMNS, rows, HEAD_DIM), f32),
-            pltpu.VMEM((1, rows, channels), bf16),
-            dma((2 + COLUMNS,)),
-            dma((1 + COLUMNS,)),
-        ],
+        scratch_shapes=[pltpu.VMEM((1, rows, channels), bf16), dma((1 + COLUMNS,))],
+        compiler_params=pltpu.CompilerParams(vmem_limit_bytes=GRANT),
         name="settle",
     )(*results)
 

time: 37.9 us -> 35.1 us (0.926)
  Pallas kernels: 37.1 us -> 34.3 us
    pallas_call x1, Pallas kernels: 35 us -> 33.3 us  [fused_shards(): pl.pallas_call(functools.partial(fused, count), out_shape=(out, jax.Shape...]
    pallas_call x1, Pallas kernels: 2.1 us -> 1 us  [fused_shards(): pl.pallas_call(settle, out_shape=(out, out), in_specs=[pl.BlockSpec(memor...]
where the time goes in v2:
time: 35.1 us; the launch traced here: 34.9 us
  Pallas kernels  34.3 us (98%)
  between operations  0.64 us (2%)
    pallas_call x1, Pallas kernels, fused_shards(): pl.pallas_call(functools.partial(fused, count), out_shape=(out, jax.Shape...  33.3 us
    pallas_call x1, Pallas kernels, fused_shards(): pl.pallas_call(settle, out_shape=(out, out), in_specs=[pl.BlockSpec(memor...  1 us

profile of v2, /device:TPU:0, one launch (start us, length us, event | category | flops | bytes accessed | tf_op | source)
XLA Modules:
  0.0 34.9 jit_solution(9011578852371696791)
XLA Ops:
  0.6 33.3 %attention.1 = (bf16[1,16,4096]{2,1,0:T(8,128)(2,1)S(1)}, bf16[3,16,4096]{2,1,0:T(8,128)(2,1)S(1)}, f32[3,2,16,128]{3,2,1,0:T(8,128)S(1)}, f32[16,2048]{1,0:T(8,128)S(1)}) custom-call(bf16[1,16,4096]{2,1,0:T(8,128)(2,1)} %self_q.1, bf16[1,16,4096]{2,1,0:T(8,128)(2,1)} %self_k.1, bf16[1,16,4096]{2,1,0:T(8,128)(2,1)} %self_v.1, bf16[1,16,4096]{2,1,0:T(8,128)(2,1)} %text_q.1, ...), custom_call_target="tpu_custom_call" | custom-call | tf_op jit(solution)/shard_map/attention/pallas_call | solution.py:600
  33.9 1.0 %settle.1 = (bf16[1,16,4096]{2,1,0:T(8,128)(2,1)}, bf16[1,16,4096]{2,1,0:T(8,128)(2,1)}) custom-call(bf16[1,16,4096]{2,1,0:T(8,128)(2,1)S(1)} %get-tuple-element.6.self_in, bf16[3,16,4096]{2,1,0:T(8,128)(2,1)S(1)} %get-tuple-element.7.text_in, f32[3,2,16,128]{3,2,1,0:T(8,128)S(1)} %get-tuple-element.8.stat_in, f32[16,2048]{1,0:T(8,128)S(1)} %get-tuple-element.9.own_in), custom_call_target="tpu_custom_call" | custom-call | tf_op jit(solution)/shard_map/settle/pallas_call | solution.py:637

commit v3 on v2

--- a/solution.py
+++ b/solution.py
@@ -142,38 +142,33 @@
 PLACES = 4
 CHUNKS = 4
 GRANT = 12 * 1024 * 1024
-SENDS = (
-    "query",
-    "relay",
-    "context",
-    "self",
-    "self_return",
-    "near",
-    "near_stat",
-    "inbound",
-    "inbound_stat",
-    "joined",
-    "joined_stat",
-)
-OUTER = ('b2', 'b4', 'b6', 'c0', 'b7', 'b5', 'b3', 'b1', 'c1', 'c2', 'c3', 'n01', 'n23', 't', 's')
-INNER = ('b6', 'r', 'b2', 'b4', 'c0', 'b7', 'b5', 'b3', 'b1', 'c1', 'n01', 'c2', 'j0', 'c3', 'n23', 'j1', 't', 's', 'j2', 'j3')
+SENDS = {"query": 0, "context": 0, "near": 0, "self": 1, "self_return": 1}
+SENDS |= {"relay": 2, "joined": 2, "inbound": 2, "near_stat": 3, "inbound_stat": 3, "joined_stat": 3}
+OUTER = ('b2', 'b4', 'b6.1', 'c0', 'b6.0', 'b7', 'b5', 'b3', 'b1', 'c1', 'c2', 'c3', 'n01', 'n23', 't', 's')
+INNER = ('b6', 'r', 'b2', 'b4.1', 'c0', 'b4.0', 'b7', 'b5', 'b3', 'b1', 'c1', 'c2', 'j0', 'c3', 'n01', 'n23', 'j1', 't', 's', 'j2', 'j3')
+FIRST_OUTER, FIRST_INNER = (), ()
 LATER = tuple(sorted(int(step[1]) for step in OUTER if step[0] == "x"))
 MESH = pl.DeviceIdType.MESH
 FAR = -1e30
 SCALE = math.log2(math.e) / math.sqrt(HEAD_DIM)
 
 
-def attend(queries, key_rows, value_rows, live):
-    scores = lax.dot_general(
-        queries, key_rows, (((1,), (1,)), ((), ())), preferred_element_type=jnp.float32
-    )
-    if live is not None:
-        scores = jnp.where(live, scores, FAR)
-    top = jnp.max(scores, axis=1, keepdims=True)
-    weights = jnp.exp2((scores - top) * SCALE)
-    total = jnp.sum(weights, axis=1, keepdims=True)
-    mixed = jnp.dot(weights.astype(jnp.bfloat16), value_rows, preferred_element_type=jnp.float32)
-    return mixed / total, top, total
+def attend(loads, heads, live):
+    scores, sides = {}, {}
+    for head in heads:
+        queries, key_rows, _ = loads(head)
+        scores[head] = lax.dot_general(
+            queries, key_rows, (((1,), (1,)), ((), ())), preferred_element_type=jnp.float32
+        )
+    for head in heads:
+        held = scores[head] if live is None else jnp.where(live, scores[head], FAR)
+        top = jnp.max(held, axis=1, keepdims=True)
+        weights = jnp.exp2((held - top) * SCALE)
+        sides[head] = weights.astype(jnp.bfloat16), top, jnp.sum(weights, axis=1, keepdims=True)
+    for head in heads:
+        weights, top, total = sides[head]
+        mixed = jnp.dot(weights, loads(head)[2], preferred_element_type=jnp.float32)
+        yield head, mixed / total, top, total
 
 
 def fused(
@@ -231,7 +226,7 @@
     self_heads, text_heads = self_span // HEAD_DIM, text_span // HEAD_DIM
     chunk_heads = text_heads // CHUNKS
     chunk_span = chunk_heads * HEAD_DIM
-    send_of = {name: sends.at[n] for n, name in enumerate(SENDS)}
+    send_of = {name: sends.at[n] for name, n in SENDS.items()}
 
     def self_cols(device):
         return pl.ds(pl.multiple_of(device * self_span, self_span), self_span)
@@ -312,6 +307,8 @@
     for chunk in range(CHUNKS):
         mine = text_q.at[0, :, part_cols(column, chunk)]
         query_copy("query", first, chunk, mine, me, across).start()
+    for chunk in range(CHUNKS):
+        mine = text_q.at[0, :, part_cols(column, chunk)]
         query_copy("query", 1, chunk, mine, me, near).start()
     def context_send(chunk):
         remote(
@@ -331,18 +328,25 @@
         for chunk in LATER:
             context_send(chunk)
 
-    for chunk in range(CHUNKS):
-        with jax.named_scope(f"q_beside{chunk}"):
-            take(held(beside, chunk), query_recv.at[0, chunk])
-        query_copy("query", first + 2, chunk, held(beside, chunk), beside, across).start()
-        query_copy("query", 1, chunk, held(beside, chunk), beside, near).start()
-
     def start_self(bits):
         to = mirror(bits)
         for kind, source in enumerate((self_q, self_k, self_v)):
             remote(
                 source.at[0, :, self_cols(to)], own.at[kind * count + me], "self", final_recv.at[3], to
             ).start()
+
+    for mask, steps in ((outer, FIRST_OUTER), (inner, FIRST_INNER)):
+
+        @pl.when(mask)
+        def _(steps=steps):
+            for step in steps:
+                start_self(int(step[1:]))
+
+    for chunk in range(CHUNKS):
+        with jax.named_scope(f"q_beside{chunk}"):
+            take(held(beside, chunk), query_recv.at[0, chunk])
+        query_copy("query", first + 2, chunk, held(beside, chunk), beside, across).start()
+        query_copy("query", 1, chunk, held(beside, chunk), beside, near).start()
 
     def far_waits(chunk):
         for n, origin in enumerate(origins):
@@ -367,10 +371,13 @@
             packed = jnp.where(lax.div(short_lane, text_heads) == n, moved, packed)
         return packed
 
+    def inbound_half(chunk, later):
+        return pl.ds(0, span) if chunk < CHUNKS - 1 else pl.ds(later * span // 2, span // 2)
+
     def join(chunk):
         with jax.named_scope(f"inb{chunk}"):
             take(stat_in.at[chunk], inbound_recv.at[1, chunk])
-            take(inbound.at[:, :, piece(chunk)], inbound_recv.at[0, chunk])
+            take(inbound.at[inbound_half(chunk, 0), :, piece(chunk)], inbound_recv.at[0, chunk])
         sides = [gathered(), stat_in[chunk]]
         highest = jnp.maximum(*sides)
         shares = [jnp.exp2(side - highest) for side in sides]
@@ -390,6 +397,8 @@
                     there + n,
                 ).start()
         for n in range(span):
+            if chunk == CHUNKS - 1 and n == span // 2:
+                take(inbound.at[inbound_half(chunk, 1), :, piece(chunk)], inbound_recv.at[0, chunk + 1])
             for head in range(chunk * chunk_heads, (chunk + 1) * chunk_heads):
                 cols = slice(head * HEAD_DIM, (head + 1) * HEAD_DIM)
                 at = n * text_heads + head
@@ -408,6 +417,16 @@
 
     neighbours = ((0, beside), (1, near), (1, near_beside))
 
+    def inbound_send(chunk, later):
+        rows_of = inbound_half(chunk, later)
+        remote(
+            text_part.at[pl.ds(there + rows_of.start, rows_of.size), :, piece(chunk)],
+            inbound.at[rows_of, :, piece(chunk)],
+            "inbound",
+            inbound_recv.at[0, chunk + later],
+            near,
+        ).start()
+
     def text_chunk(chunk, role):
         if role == "outer":
             for _n in far_waits(chunk):
@@ -417,27 +436,25 @@
         with jax.named_scope(f"kv{chunk}"):
             take(context.at[0, :, :, piece(chunk)], context_recv.at[chunk])
         tops, totals = jnp.full((query_total, HEAD_DIM), FAR, jnp.float32), 1.0
-        for head in range(chunk * chunk_heads, (chunk + 1) * chunk_heads):
+
+        def loads(head):
             cols = slice(head * HEAD_DIM, (head + 1) * HEAD_DIM)
-            mixed, top, total = attend(
+            return (
                 text_rows[:, :, cols].reshape(query_total, HEAD_DIM),
                 context[:, 0, :, cols].reshape(key_total, HEAD_DIM),
                 context[:, 1, :, cols].reshape(key_total, HEAD_DIM),
-                live,
             )
+
+        heads = range(chunk * chunk_heads, (chunk + 1) * chunk_heads)
+        for head, mixed, top, total in attend(loads, heads, live):
+            cols = slice(head * HEAD_DIM, (head + 1) * HEAD_DIM)
             share = mixed.reshape(count, rows, HEAD_DIM)
             text_full[:, :, cols] = share
             text_part[:, :, cols] = share.astype(jnp.bfloat16)
             tops = jnp.where(lane == head, top, tops)
             totals = jnp.where(lane == head, total, totals)
         if role == "outer":
-            remote(
-                text_part.at[pl.ds(there, span), :, piece(chunk)],
-                inbound.at[:, :, piece(chunk)],
-                "inbound",
-                inbound_recv.at[0, chunk],
-                near,
-            ).start()
+            inbound_send(chunk, 0)
         levels = (tops * SCALE + jnp.log2(totals)).reshape(count, rows, HEAD_DIM)
         if chunk:
             before = lax.broadcasted_iota(jnp.int32, (1, 1, HEAD_DIM), 2) < chunk * chunk_heads
@@ -448,6 +465,8 @@
             remote(
                 stat_pack.at[chunk], stat_in.at[chunk], "inbound_stat", inbound_recv.at[1, chunk], near
             ).start()
+            if chunk == CHUNKS - 1:
+                inbound_send(chunk, 1)
 
     def near_send(low, high):
         for slot, device in neighbours:
@@ -469,14 +488,16 @@
         take(own.at[pl.ds(0, 3)], local_sem.at[2])
         with jax.named_scope("self"):
             take(own.at[pl.ds(0, 3 * (count - 1))], final_recv.at[3])
-        for head in range(self_heads):
+
+        def loads(head):
             cols = slice(head * HEAD_DIM, (head + 1) * HEAD_DIM)
-            mixed, _, _ = attend(
-                own[0:count, :, cols].reshape(query_total, HEAD_DIM),
-                own[count : 2 * count, :, cols].reshape(query_total, HEAD_DIM),
-                own[2 * count : 3 * count, :, cols].reshape(query_total, HEAD_DIM),
-                None,
-            )
+            return [
+                own[kind * count : (kind + 1) * count, :, cols].reshape(query_total, HEAD_DIM)
+                for kind in range(3)
+            ]
+
+        for head, mixed, _, _ in attend(loads, range(self_heads), None):
+            cols = slice(head * HEAD_DIM, (head + 1) * HEAD_DIM)
             self_part[:, :, cols] = mixed.astype(jnp.bfloat16).reshape(count, rows, HEAD_DIM)
         for n in range(count - 1):
             to = n + lax.div(n + count - me, count)
@@ -535,23 +556,17 @@
     with jax.named_scope("self_out"):
         take(self_part.at[pl.ds(0, count - 1)], final_recv.at[2])
     with jax.named_scope("sends"):
-        take(text_rows.at[pl.ds(0, 5)], send_of["query"])
-        take(context.at[0], send_of["context"])
-        take(own.at[pl.ds(0, 3 * (count - 1))], send_of["self"])
-        take(self_part.at[pl.ds(0, count - 1)], send_of["self_return"])
-        take(text_part.at[pl.ds(0, 3)], send_of["near"])
-        take(stat_part.at[pl.ds(0, 3)], send_of["near_stat"])
+        take(text_full, sends.at[0])
+        take(text_rows.at[pl.ds(0, count - 1)], sends.at[1])
+        take(stat_part.at[pl.ds(0, count - 1)], sends.at[3])
 
     @pl.when(outer)
     def _():
-        take(inbound, send_of["inbound"])
-        take(stat_pack, send_of["inbound_stat"])
+        take(inbound, sends.at[2])
 
     @pl.when(inner)
     def _():
-        take(text_rows.at[pl.ds(0, span)], send_of["relay"])
-        take(joined, send_of["joined"])
-        take(stat_join, send_of["joined_stat"])
+        take(text_rows, sends.at[2])
 
 
 def settle(self_in, text_in, stat_in, own_in, self_out, text_out, mixed, out_sem):
@@ -624,9 +639,9 @@
             pltpu.SMEM(text_len.shape, jnp.int32),
             dma((2 + span, CHUNKS)),
             dma((CHUNKS,)),
-            dma((2, CHUNKS)),
+            dma((2, CHUNKS + 1)),
             dma((4,)),
-            dma((len(SENDS),)),
+            dma((4,)),
             dma((4,)),
         ],
         compiler_params=pltpu.CompilerParams(

time: 35.1 us -> 34.6 us (0.986)
  Pallas kernels: 34.3 us -> 33.9 us
    pallas_call x1, Pallas kernels: 33.3 us -> 32.9 us  [fused_shards(): pl.pallas_call(functools.partial(fused, count), out_shape=(out, jax.Shape...]
where the time goes in v3:
time: 34.6 us; the launch traced here: 34.5 us
  Pallas kernels  33.9 us (98%)
  between operations  0.64 us (2%)
    pallas_call x1, Pallas kernels, fused_shards(): pl.pallas_call(functools.partial(fused, count), out_shape=(out, jax.Shape...  32.9 us
    pallas_call x1, Pallas kernels, fused_shards(): pl.pallas_call(settle, out_shape=(out, out), in_specs=[pl.BlockSpec(memor...  1 us

profile of v3, /device:TPU:0, one launch (start us, length us, event | category | flops | bytes accessed | tf_op | source)
XLA Modules:
  0.0 34.5 jit_solution(17938977708986821374)
XLA Ops:
  0.6 32.9 %attention.1 = (bf16[1,16,4096]{2,1,0:T(8,128)(2,1)S(1)}, bf16[3,16,4096]{2,1,0:T(8,128)(2,1)S(1)}, f32[3,2,16,128]{3,2,1,0:T(8,128)S(1)}, f32[16,2048]{1,0:T(8,128)S(1)}) custom-call(bf16[1,16,4096]{2,1,0:T(8,128)(2,1)} %self_q.1, bf16[1,16,4096]{2,1,0:T(8,128)(2,1)} %self_k.1, bf16[1,16,4096]{2,1,0:T(8,128)(2,1)} %self_v.1, bf16[1,16,4096]{2,1,0:T(8,128)(2,1)} %text_q.1, ...), custom_call_target="tpu_custom_call" | custom-call | tf_op jit(solution)/shard_map/attention/pallas_call | solution.py:615
  33.5 1.0 %settle.1 = (bf16[1,16,4096]{2,1,0:T(8,128)(2,1)}, bf16[1,16,4096]{2,1,0:T(8,128)(2,1)}) custom-call(bf16[1,16,4096]{2,1,0:T(8,128)(2,1)S(1)} %get-tuple-element.6.self_in, bf16[3,16,4096]{2,1,0:T(8,128)(2,1)S(1)} %get-tuple-element.7.text_in, f32[3,2,16,128]{3,2,1,0:T(8,128)S(1)} %get-tuple-element.8.stat_in, f32[16,2048]{1,0:T(8,128)S(1)} %get-tuple-element.9.own_in), custom_call_target="tpu_custom_call" | custom-call | tf_op jit(solution)/shard_map/settle/pallas_call | solution.py:652

commit v4 on v3

--- a/solution.py
+++ b/solution.py
@@ -144,8 +144,8 @@
 GRANT = 12 * 1024 * 1024
 SENDS = {"query": 0, "context": 0, "near": 0, "self": 1, "self_return": 1}
 SENDS |= {"relay": 2, "joined": 2, "inbound": 2, "near_stat": 3, "inbound_stat": 3, "joined_stat": 3}
-OUTER = ('b2', 'b4', 'b6.1', 'c0', 'b6.0', 'b7', 'b5', 'b3', 'b1', 'c1', 'c2', 'c3', 'n01', 'n23', 't', 's')
-INNER = ('b6', 'r', 'b2', 'b4.1', 'c0', 'b4.0', 'b7', 'b5', 'b3', 'b1', 'c1', 'c2', 'j0', 'c3', 'n01', 'n23', 'j1', 't', 's', 'j2', 'j3')
+OUTER = ('b2.0', 'b2.1', 'b4.0', 'b6.1', 'c0', 'b6.0', 'b4.1', 'b7.0', 'b7.1', 'b5.0', 'b5.1', 'b3.1', 'b1.0', 'b1.1', 'b3.0', 'c1', 'c2', 'c3', 't.h0', 'n01.h0', 'n23.h0', 's', 'n01.h1', 'n23.h1', 't.h1')
+INNER = ('b6', 'r', 'b2', 'b4.1', 'c0', 'b4.0', 'b7', 'b5', 'b3', 'b1', 'c1', 'n01.h0', 'c2', 'n22.h0', 'j0', 'c3', 't.h0', 'n33.h0', 'j1', 's', 'j2', 'j3', 'n01.h1', 'n23.h1', 't.h1')
 FIRST_OUTER, FIRST_INNER = (), ()
 LATER = tuple(sorted(int(step[1]) for step in OUTER if step[0] == "x"))
 MESH = pl.DeviceIdType.MESH
@@ -415,7 +415,10 @@
                 there + n,
             ).start()
 
-    neighbours = ((0, beside), (1, near), (1, near_beside))
+    neighbours = (
+        *((1, COLUMNS * near_place + side) for side in range(COLUMNS)),
+        (0, beside),
+    )
 
     def inbound_send(chunk, later):
         rows_of = inbound_half(chunk, later)
@@ -525,7 +528,8 @@
                 "s": self_attention,
             }[kind]
             if only:
-                pl.when(branch == int(only))(functools.partial(action, *digits))
+                holds = half == int(only[1:]) if only[0] == "h" else branch == int(only)
+                pl.when(holds)(functools.partial(action, *digits))
             else:
                 action(*digits)
 

time: 34.6 us -> 34.4 us (level)
  no operation moved by 1% of the time
where the time goes in v4:
time: 34.4 us; the launch traced here: 34.3 us
  Pallas kernels  33.6 us (98%)
  between operations  0.64 us (2%)
    pallas_call x1, Pallas kernels, fused_shards(): pl.pallas_call(functools.partial(fused, count), out_shape=(out, jax.Shape...  32.6 us
    pallas_call x1, Pallas kernels, fused_shards(): pl.pallas_call(settle, out_shape=(out, out), in_specs=[pl.BlockSpec(memor...  1 us

profile of v4, /device:TPU:0, one launch (start us, length us, event | category | flops | bytes accessed | tf_op | source)
XLA Modules:
  0.0 34.3 jit_solution(8676496253352508224)
XLA Ops:
  0.6 32.6 %attention.1 = (bf16[1,16,4096]{2,1,0:T(8,128)(2,1)S(1)}, bf16[3,16,4096]{2,1,0:T(8,128)(2,1)S(1)}, f32[3,2,16,128]{3,2,1,0:T(8,128)S(1)}, f32[16,2048]{1,0:T(8,128)S(1)}) custom-call(bf16[1,16,4096]{2,1,0:T(8,128)(2,1)} %self_q.1, bf16[1,16,4096]{2,1,0:T(8,128)(2,1)} %self_k.1, bf16[1,16,4096]{2,1,0:T(8,128)(2,1)} %self_v.1, bf16[1,16,4096]{2,1,0:T(8,128)(2,1)} %text_q.1, ...), custom_call_target="tpu_custom_call" | custom-call | tf_op jit(solution)/shard_map/attention/pallas_call | solution.py:619
  33.3 1.0 %settle.1 = (bf16[1,16,4096]{2,1,0:T(8,128)(2,1)}, bf16[1,16,4096]{2,1,0:T(8,128)(2,1)}) custom-call(bf16[1,16,4096]{2,1,0:T(8,128)(2,1)S(1)} %get-tuple-element.6.self_in, bf16[3,16,4096]{2,1,0:T(8,128)(2,1)S(1)} %get-tuple-element.7.text_in, f32[3,2,16,128]{3,2,1,0:T(8,128)S(1)} %get-tuple-element.8.stat_in, f32[16,2048]{1,0:T(8,128)S(1)} %get-tuple-element.9.own_in), custom_call_target="tpu_custom_call" | custom-call | tf_op jit(solution)/shard_map/settle/pallas_call | solution.py:656

commit v5 on v4

--- a/solution.py
+++ b/solution.py
@@ -271,19 +271,6 @@
         pl.semaphore_signal(
             barrier, inc=1, device_id={"seq": lax.rem(me + step, count)}, device_id_type=MESH
         )
-    kept_len = pltpu.make_async_copy(text_len, live_len, local_sem.at[3])
-    kept_rows = pltpu.make_async_copy(text_q.at[0, :, text_cols(column)], text_rows.at[me], local_sem.at[0])
-    kept_context = pltpu.make_async_copy(
-        text_kv.at[0, :, :, text_cols(column)], context.at[column], local_sem.at[1]
-    )
-    kept_len.start()
-    kept_rows.start()
-    kept_context.start()
-    for kind, source in enumerate((self_q, self_k, self_v)):
-        pltpu.make_async_copy(
-            source.at[0, :, self_cols(me)], own.at[kind * count + me], local_sem.at[2]
-        ).start()
-
     with jax.named_scope("entry"):
         pl.semaphore_wait(barrier, count - 1)
 
@@ -327,6 +314,19 @@
     def _():
         for chunk in LATER:
             context_send(chunk)
+
+    kept_len = pltpu.make_async_copy(text_len, live_len, local_sem.at[3])
+    kept_rows = pltpu.make_async_copy(text_q.at[0, :, text_cols(column)], text_rows.at[me], local_sem.at[0])
+    kept_context = pltpu.make_async_copy(
+        text_kv.at[0, :, :, text_cols(column)], context.at[column], local_sem.at[1]
+    )
+    kept_len.start()
+    kept_rows.start()
+    kept_context.start()
+    for kind, source in enumerate((self_q, self_k, self_v)):
+        pltpu.make_async_copy(
+            source.at[0, :, self_cols(me)], own.at[kind * count + me], local_sem.at[2]
+        ).start()
 
     def start_self(bits):
         to = mirror(bits)

time: 34.4 us -> 34.4 us (level)
  no operation moved by 1% of the time
where the time goes in v5:
time: 34.4 us; the launch traced here: 34.3 us
  Pallas kernels  33.6 us (98%)
  between operations  0.64 us (2%)
    pallas_call x1, Pallas kernels, fused_shards(): pl.pallas_call(functools.partial(fused, count), out_shape=(out, jax.Shape...  32.6 us
    pallas_call x1, Pallas kernels, fused_shards(): pl.pallas_call(settle, out_shape=(out, out), in_specs=[pl.BlockSpec(memor...  1 us

profile of v5, /device:TPU:0, one launch (start us, length us, event | category | flops | bytes accessed | tf_op | source)
XLA Modules:
  0.0 34.3 jit_solution(727287101597860202)
XLA Ops:
  0.6 32.6 %attention.1 = (bf16[1,16,4096]{2,1,0:T(8,128)(2,1)S(1)}, bf16[3,16,4096]{2,1,0:T(8,128)(2,1)S(1)}, f32[3,2,16,128]{3,2,1,0:T(8,128)S(1)}, f32[16,2048]{1,0:T(8,128)S(1)}) custom-call(bf16[1,16,4096]{2,1,0:T(8,128)(2,1)} %self_q.1, bf16[1,16,4096]{2,1,0:T(8,128)(2,1)} %self_k.1, bf16[1,16,4096]{2,1,0:T(8,128)(2,1)} %self_v.1, bf16[1,16,4096]{2,1,0:T(8,128)(2,1)} %text_q.1, ...), custom_call_target="tpu_custom_call" | custom-call | tf_op jit(solution)/shard_map/attention/pallas_call | solution.py:619
  33.3 1.0 %settle.1 = (bf16[1,16,4096]{2,1,0:T(8,128)(2,1)}, bf16[1,16,4096]{2,1,0:T(8,128)(2,1)}) custom-call(bf16[1,16,4096]{2,1,0:T(8,128)(2,1)S(1)} %get-tuple-element.6.self_in, bf16[3,16,4096]{2,1,0:T(8,128)(2,1)S(1)} %get-tuple-element.7.text_in, f32[3,2,16,128]{3,2,1,0:T(8,128)S(1)} %get-tuple-element.8.stat_in, f32[16,2048]{1,0:T(8,128)S(1)} %get-tuple-element.9.own_in), custom_call_target="tpu_custom_call" | custom-call | tf_op jit(solution)/shard_map/settle/pallas_call | solution.py:656

commit v6 on v5

--- a/solution.py
+++ b/solution.py
@@ -141,6 +141,7 @@
 HALVES = 2
 PLACES = 4
 CHUNKS = 4
+WRITE_HEADS = 8
 GRANT = 12 * 1024 * 1024
 SENDS = {"query": 0, "context": 0, "near": 0, "self": 1, "self_return": 1}
 SENDS |= {"relay": 2, "joined": 2, "inbound": 2, "near_stat": 3, "inbound_stat": 3, "joined_stat": 3}
@@ -596,11 +597,13 @@
                 for n in range(1, HALVES + 1)
             )
             mixed[0, :, cols] = merged.astype(jnp.bfloat16)
-        piece = pl.ds(side * text_span, text_span)
-        leaving.append(
-            pltpu.make_async_copy(mixed.at[:, :, piece], text_out.at[:, :, piece], out_sem.at[1 + side])
-        )
-        leaving[1 + side].start()
+            if (head + 1) % WRITE_HEADS == 0:
+                piece = pl.ds(cols.stop - WRITE_HEADS * HEAD_DIM, WRITE_HEADS * HEAD_DIM)
+                copy = pltpu.make_async_copy(
+                    mixed.at[:, :, piece], text_out.at[:, :, piece], out_sem.at[len(leaving)]
+                )
+                copy.start()
+                leaving.append(copy)
     for copy in leaving:
         copy.wait()
 
@@ -658,7 +661,7 @@
         out_shape=(out, out),
         in_specs=[pl.BlockSpec(memory_space=pltpu.VMEM)] * 4,
         out_specs=(in_place, in_place),
-        scratch_shapes=[pltpu.VMEM((1, rows, channels), bf16), dma((1 + COLUMNS,))],
+        scratch_shapes=[pltpu.VMEM((1, rows, channels), bf16), dma((1 + HEADS // WRITE_HEADS,))],
         compiler_params=pltpu.CompilerParams(vmem_limit_bytes=GRANT),
         name="settle",
     )(*results)

time: 34.4 us -> 34.4 us (level)
  no operation moved by 1% of the time
where the time goes in v6:
time: 34.4 us; the launch traced here: 34.3 us
  Pallas kernels  33.6 us (98%)
  between operations  0.64 us (2%)
    pallas_call x1, Pallas kernels, fused_shards(): pl.pallas_call(functools.partial(fused, count), out_shape=(out, jax.Shape...  32.6 us
    pallas_call x1, Pallas kernels, fused_shards(): pl.pallas_call(settle, out_shape=(out, out), in_specs=[pl.BlockSpec(memor...  1 us

profile of v6, /device:TPU:0, one launch (start us, length us, event | category | flops | bytes accessed | tf_op | source)
XLA Modules:
  0.0 34.3 jit_solution(4114665317652402624)
XLA Ops:
  0.6 32.6 %attention.1 = (bf16[1,16,4096]{2,1,0:T(8,128)(2,1)S(1)}, bf16[3,16,4096]{2,1,0:T(8,128)(2,1)S(1)}, f32[3,2,16,128]{3,2,1,0:T(8,128)S(1)}, f32[16,2048]{1,0:T(8,128)S(1)}) custom-call(bf16[1,16,4096]{2,1,0:T(8,128)(2,1)} %self_q.1, bf16[1,16,4096]{2,1,0:T(8,128)(2,1)} %self_k.1, bf16[1,16,4096]{2,1,0:T(8,128)(2,1)} %self_v.1, bf16[1,16,4096]{2,1,0:T(8,128)(2,1)} %text_q.1, ...), custom_call_target="tpu_custom_call" | custom-call | tf_op jit(solution)/shard_map/attention/pallas_call | solution.py:622
  33.3 1.0 %settle.1 = (bf16[1,16,4096]{2,1,0:T(8,128)(2,1)}, bf16[1,16,4096]{2,1,0:T(8,128)(2,1)}) custom-call(bf16[1,16,4096]{2,1,0:T(8,128)(2,1)S(1)} %get-tuple-element.6.self_in, bf16[3,16,4096]{2,1,0:T(8,128)(2,1)S(1)} %get-tuple-element.7.text_in, f32[3,2,16,128]{3,2,1,0:T(8,128)S(1)} %get-tuple-element.8.stat_in, f32[16,2048]{1,0:T(8,128)S(1)} %get-tuple-element.9.own_in), custom_call_target="tpu_custom_call" | custom-call | tf_op jit(solution)/shard_map/settle/pallas_call | solution.py:659

commit v7 on v6

--- a/solution.py
+++ b/solution.py
@@ -146,7 +146,7 @@
 SENDS = {"query": 0, "context": 0, "near": 0, "self": 1, "self_return": 1}
 SENDS |= {"relay": 2, "joined": 2, "inbound": 2, "near_stat": 3, "inbound_stat": 3, "joined_stat": 3}
 OUTER = ('b2.0', 'b2.1', 'b4.0', 'b6.1', 'c0', 'b6.0', 'b4.1', 'b7.0', 'b7.1', 'b5.0', 'b5.1', 'b3.1', 'b1.0', 'b1.1', 'b3.0', 'c1', 'c2', 'c3', 't.h0', 'n01.h0', 'n23.h0', 's', 'n01.h1', 'n23.h1', 't.h1')
-INNER = ('b6', 'r', 'b2', 'b4.1', 'c0', 'b4.0', 'b7', 'b5', 'b3', 'b1', 'c1', 'n01.h0', 'c2', 'n22.h0', 'j0', 'c3', 't.h0', 'n33.h0', 'j1', 's', 'j2', 'j3', 'n01.h1', 'n23.h1', 't.h1')
+INNER = ('b6', 'r', 'b2', 'b4.1', 'c0', 'b4.0', 'b7', 'b5', 'b3', 'b1', 'c1', 'n01.h0', 'c2', 'n22.h0', 'j0', 'c3', 't.h0', 'n33.h0', 'j1', 'j2', 's', 'j3', 'n01.h1', 'n23.h1', 't.h1')
 FIRST_OUTER, FIRST_INNER = (), ()
 LATER = tuple(sorted(int(step[1]) for step in OUTER if step[0] == "x"))
 MESH = pl.DeviceIdType.MESH

time: 34.4 us -> 34.5 us (level)
  no operation moved by 1% of the time
where the time goes in v7:
time: 34.5 us; the launch traced here: 34.3 us
  Pallas kernels  33.7 us (98%)
  between operations  0.64 us (2%)
    pallas_call x1, Pallas kernels, fused_shards(): pl.pallas_call(functools.partial(fused, count), out_shape=(out, jax.Shape...  32.7 us
    pallas_call x1, Pallas kernels, fused_shards(): pl.pallas_call(settle, out_shape=(out, out), in_specs=[pl.BlockSpec(memor...  1 us

profile of v7, /device:TPU:0, one launch (start us, length us, event | category | flops | bytes accessed | tf_op | source)
XLA Modules:
  0.0 34.3 jit_solution(2449019640965235998)
XLA Ops:
  0.6 32.7 %attention.1 = (bf16[1,16,4096]{2,1,0:T(8,128)(2,1)S(1)}, bf16[3,16,4096]{2,1,0:T(8,128)(2,1)S(1)}, f32[3,2,16,128]{3,2,1,0:T(8,128)S(1)}, f32[16,2048]{1,0:T(8,128)S(1)}) custom-call(bf16[1,16,4096]{2,1,0:T(8,128)(2,1)} %self_q.1, bf16[1,16,4096]{2,1,0:T(8,128)(2,1)} %self_k.1, bf16[1,16,4096]{2,1,0:T(8,128)(2,1)} %self_v.1, bf16[1,16,4096]{2,1,0:T(8,128)(2,1)} %text_q.1, ...), custom_call_target="tpu_custom_call" | custom-call | tf_op jit(solution)/shard_map/attention/pallas_call | solution.py:622
  33.3 1.0 %settle.1 = (bf16[1,16,4096]{2,1,0:T(8,128)(2,1)}, bf16[1,16,4096]{2,1,0:T(8,128)(2,1)}) custom-call(bf16[1,16,4096]{2,1,0:T(8,128)(2,1)S(1)} %get-tuple-element.6.self_in, bf16[3,16,4096]{2,1,0:T(8,128)(2,1)S(1)} %get-tuple-element.7.text_in, f32[3,2,16,128]{3,2,1,0:T(8,128)S(1)} %get-tuple-element.8.stat_in, f32[16,2048]{1,0:T(8,128)S(1)} %get-tuple-element.9.own_in), custom_call_target="tpu_custom_call" | custom-call | tf_op jit(solution)/shard_map/settle/pallas_call | solution.py:659
